TPU v7x, 32 devices: a whole 2x2x4 slice. The times are simulated.
32 devices in a mesh: grp: 2 (over y), band: 8 (over z, x), rcv: 2 (over core).
Axes of the slice: x: 2, y: 2, z: 4, core: 2. Of those that a mesh axis runs over, the one named last changes fastest.
Arguments:
- traces: bfloat16 [2048, 1024, 256], P(('grp', 'band'), 'rcv'), parts along dimension 0, may hold values from -6 to 6
Outputs:
- multiples: bfloat16 [2048, 1024, 256], P(('grp', 'band'), 'rcv'), parts along dimension 0
There are 2 independent parts, one for each index of `grp`. A program takes and returns all parts, laid end to end along the dimension named above; each array names one. Nothing has to cross between parts.
All inputs are finite; a program needn't handle non-finite values.
Results may differ from a plain program's by a relative error of at most 0.0082.
Values may be sent and summed in bfloat16 or wider, within the bound.
No kernel may reach another device: no remote copies, remote signals or barrier semaphores. Data moves between devices by JAX's collectives and lax.ppermute only.
A program may use at most 384 MiB of HBM per device.

v0:
```python
import math

import jax
import jax.numpy as jnp
from jax import lax
from jax.sharding import PartitionSpec as P


def tables(length):
    times_int = jnp.arange(length, dtype=jnp.int32)
    freqs_int = jnp.arange(length // 2, dtype=jnp.int32)
    phase_int = times_int[:, None] * freqs_int[None, :] % length
    angles = phase_int.astype(jnp.float32) * jnp.float32(2.0 * math.pi / length)
    factor = jnp.float32(1.0 / math.sqrt(length))
    cosine = jnp.cos(angles) * factor
    sine_part = jnp.sin(angles) * factor
    forward = jnp.stack([cosine, -sine_part], axis=2).reshape(length, length).astype(jnp.bfloat16)
    weights = jnp.where(freqs_int == 0, 1.0, 2.0).astype(jnp.float32)
    inverse = jnp.stack(
        [cosine.T * weights[:, None], -sine_part.T * weights[:, None]], axis=1
    ).astype(jnp.bfloat16)
    return (forward, inverse)


def complex_right(rows_part):
    real_part = rows_part[:, 0]
    imag_part = rows_part[:, 1]
    first_row = jnp.stack([real_part, imag_part], axis=1)
    second_row = jnp.stack([-imag_part, real_part], axis=1)
    return jnp.stack([first_row, second_row], axis=1)


def complex_product(left_part, rows_part):
    return jnp.einsum(
        "fqsk,fqpkr->fpsr", left_part, complex_right(rows_part), preferred_element_type=jnp.float32
    )


def body(traces):
    length = traces.shape[2]
    stations = traces.shape[0] * lax.axis_size("band")
    factor = jnp.float32(1.0 / math.sqrt(stations))
    forward, inverse = tables(length)
    spectra = jnp.einsum("srt,tc->csr", traces, forward, preferred_element_type=jnp.float32).astype(
        jnp.bfloat16
    )
    owned_spec = lax.all_to_all(spectra, "band", split_axis=0, concat_axis=1, tiled=True)
    channels = owned_spec.shape[0]
    owned_spec = owned_spec.reshape(channels // 2, 2, owned_spec.shape[1], owned_spec.shape[2])
    receiver_panel = lax.all_to_all(owned_spec, "rcv", split_axis=2, concat_axis=3, tiled=True)
    block_terms = complex_product(owned_spec, receiver_panel) * factor
    summed = lax.psum_scatter(
        block_terms.astype(jnp.bfloat16), "rcv", scatter_dimension=3, tiled=True
    )
    source_spec = lax.all_to_all(summed, "band", split_axis=2, concat_axis=0, tiled=True)
    result = jnp.einsum("fpsr,fpt->srt", source_spec, inverse, preferred_element_type=jnp.float32)
    return result.astype(jnp.bfloat16)


def solution(mesh):
    placed = (P(("grp", "band"), "rcv", None),)
    return jax.shard_map(
        body, mesh=mesh, in_specs=placed, out_specs=P(("grp", "band"), "rcv", None), check_vma=False
    )
```

profile of v0, /device:TPU:11, one launch (start us, length us, event | category | flops | bytes accessed | tf_op | source)
XLA Modules:
  0.0 2174.7 jit_solution(14784228975921841595)
XLA Ops:
  6.5 0.0 reduce-scatter.2.cloned.1.call-start
  6.5 0.5 negate_convert_fusion
  7.1 0.1 copy.33
  7.3 0.1 reshape.206
  7.3 26.4 %convolution_convert_fusion = bf16[256,128,512]{2,0,1:T(8,128)(2,1)} fusion(bf16[256,256,1]{0,1,2:T(8,128)(2,1)S(1)} %reshape.206, bf16[128,512,256]{2,1,0:T(8,128)(2,1)} %param.1), kind=kOutput, calls=%fused_computation.11 | convolution fusion | flops 8606711808 | bytes 67239936 | tf_op jit(solution)/shard_map/srt,tc->csr/dot_general | solution.py:44
  33.7 31.1 %copy.34 = bf16[256,128,512]{2,1,0:T(8,128)(2,1)} copy(bf16[256,128,512]{2,0,1:T(8,128)(2,1)} %convolution_convert_fusion) | data formatting | bytes 67108864 | tf_op jit(solution)/shard_map/convert_element_type | solution.py:44
  64.8 730.6 %all_to_all.51 = bf16[256,128,512]{2,1,0:T(8,128)(2,1)} all-to-all(bf16[256,128,512]{2,1,0:T(8,128)(2,1)} %copy.34), channel_id=1, replica_groups=mesh['grp'=2,'band'=8,'rcv'=2] {'band'}, dimensions={0} | all-to-all | bytes 67108864 | tf_op jit(solution)/shard_map/all_to_all | solution.py:47
  795.4 23.0 %copy.35 = bf16[8,32,128,512]{3,2,0,1:T(8,128)(2,1)} copy(bf16[8,32,128,512]{3,2,1,0:T(8,128)(2,1)} %bitcast.47) | data formatting | bytes 67108864 | tf_op jit(solution)/shard_map/all_to_all | solution.py:47
  818.4 60.1 %copy.36 = bf16[16,2,1024,512]{3,1,0,2:T(2,128)(2,1)} copy(bf16[16,2,1024,512]{3,2,1,0:T(8,128)(2,1)} %bitcast.43) | data formatting | bytes 67108864 | tf_op jit(solution)/shard_map/reshape | solution.py:49
  878.5 59.4 %all_to_all.52 = bf16[16,2,1024,512]{3,1,0,2:T(2,128)(2,1)} all-to-all(bf16[16,2,1024,512]{3,1,0,2:T(2,128)(2,1)} %copy.36), channel_id=1, replica_groups=mesh['grp'=2,'band'=8,'rcv'=2] {'rcv'}, dimensions={2} | all-to-all | bytes 67108864 | tf_op jit(solution)/shard_map/all_to_all | solution.py:50
  938.0 80.3 %copy.37 = bf16[16,2,2,512,512]{3,4,2,1,0:T(8,128)(2,1)} copy(bf16[16,2,2,512,512]{4,1,0,3,2:T(2,128)(2,1)} %bitcast.48) | data formatting | bytes 67108864 | tf_op jit(solution)/shard_map/all_to_all | solution.py:50
  1018.3 22.5 %slice_negate_fusion = (bf16[16,1,512,1024]{2,3,1,0:T(8,128)(2,1)}, bf16[16,1,512,1024]{2,3,1,0:T(8,128)(2,1)}) fusion(bf16[16,2,512,1024]{2,3,1,0:T(8,128)(2,1)} %bitcast.45), kind=kLoop, calls=%fused_computation.12 | loop fusion | flops 8388608 | bytes 67108864 | tf_op jit(solution)/shard_map/neg | solution.py:29
  1040.8 22.9 %maximum_bitcast_fusion = bf16[16,1,2,512,1024]{3,4,1,2,0:T(8,128)(2,1)} fusion(bf16[16,1,512,1024]{2,3,1,0:T(8,128)(2,1)} %get-tuple-element.6, bf16[16,1,512,1024]{2,3,1,0:T(8,128)(2,1)} %get-tuple-element.5), kind=kLoop, calls=%fused_computation.8 | loop fusion | flops 16777216 | bytes 67108864 | tf_op jit(solution)/shard_map/stack | solution.py:30
  1063.7 88.8 %fusion.1 = bf16[16,2,1024,1024]{2,3,1,0:T(8,128)(2,1)} fusion(bf16[16,2,1024,512,1]{3,2,1,4,0:T(8,128)(2,1)} %bitcast.44, bf16[16,1,2,512,1024]{3,4,1,2,0:T(8,128)(2,1)} %maximum_bitcast_fusion, bf16[16,1,2,512,1024]{3,4,1,2,0:T(8,128)(2,1)} %bitcast.46), kind=kOutput, calls=%fused_computation.2 | convolution fusion | flops 68820140032 | bytes 167772160 | tf_op jit(solution)/shard_map/fqsk,fqpkr->fpsr/dot_general | solution.py:34
  1152.6 0.0 reduce-scatter.2.cloned.1.call-update
  1152.6 84.2 %reduce-scatter.2.cloned.1.call-done = bf16[16,2,1024,512]{2,3,1,0:T(8,128)(2,1)} async-done(((bf16[16,2,1024,1024]{2,3,1,0:T(8,128)(2,1)}), bf16[16,2,1024,512]{2,3,1,0:T(8,128)(2,1)}) %reduce-scatter.2.cloned.1.call-update) | async-done | bytes 33554448 | tf_op jit(solution)/shard_map/reduce_scatter | solution.py:52
  1236.8 80.4 %copy.38 = bf16[16,2,1024,512]{3,1,0,2:T(2,128)(2,1)} copy(bf16[16,2,1024,512]{2,3,1,0:T(8,128)(2,1)} %reduce-scatter.2.cloned.1.call-done) | data formatting | bytes 67108864 | tf_op jit(solution)/shard_map/reduce_scatter | solution.py:52
  1317.3 7.0 all-to-all-start.2
  1324.3 0.6 multiply_convert_fusion
  1324.9 719.1 %all-to-all-done.2 = bf16[16,2,1024,512]{3,1,0,2:T(2,128)(2,1)} async-done(((bf16[16,2,1024,512]{3,1,0,2:T(2,128)(2,1)}), bf16[16,2,1024,512]{3,1,0,2:T(2,128)(2,1)}, u32[]{:S(2)}, u32[]{:S(2)}) %all-to-all-start.2) | async-done | bytes 33554464 | tf_op jit(solution)/shard_map/all_to_all | solution.py:55
  2044.0 23.4 %copy.39 = bf16[16,2,1024,512]{3,2,1,0:T(8,128)(2,1)} copy(bf16[16,2,1024,512]{3,1,0,2:T(2,128)(2,1)} %all-to-all-done.2) | data formatting | bytes 67108864 | tf_op jit(solution)/shard_map/all_to_all | solution.py:55
  2067.4 23.0 %copy.40 = bf16[8,16,2,128,512]{4,3,2,1,0:T(8,128)(2,1)} copy(bf16[8,16,2,128,512]{4,3,0,2,1:T(8,128)(2,1)} %bitcast.49) | data formatting | bytes 67108864 | tf_op jit(solution)/shard_map/all_to_all | solution.py:55
  2090.4 77.5 %bitcast_convert_fusion = bf16[128,512,256]{2,1,0:T(8,128)(2,1)} fusion(bf16[128,2,128,512]{3,2,1,0:T(8,128)(2,1)} %bitcast.50, bf16[128,1,256]{2,0,1:T(8,128)(2,1)S(1)} %get-tuple-element.9, bf16[128,1,256]{2,0,1:T(8,128)(2,1)S(1)} %get-tuple-element.10), kind=kOutput, calls=%fused_computation.7 | convolution fusion | flops 8606777344 | bytes 67239936 | tf_op jit(solution)/shard_map/fpsr,fpt->srt/dot_general | solution.py:56
  (3 shorter events, 0.0 us)
Async XLA Ops:
  6.5 1230.3 %reduce-scatter.2.cloned.1.call-start = ((), (), s32[]{:S(2)}) async-start(), calls=%async_computation.4 | async-start | bytes 100663296 | tf_op jit(solution)/shard_map/reduce_scatter | solution.py:52
  1317.3 726.8 %all-to-all-start.2 = ((bf16[16,2,1024,512]{3,1,0,2:T(2,128)(2,1)}), bf16[16,2,1024,512]{3,1,0,2:T(2,128)(2,1)}, u32[]{:S(2)}, u32[]{:S(2)}) async-start(bf16[16,2,1024,512]{3,1,0,2:T(2,128)(2,1)} %copy.38), calls=%async_computation.3 | async-start | bytes 67108864 | tf_op jit(solution)/shard_map/all_to_all | solution.py:55
Sparse Core Ops, SparseCore 0:
  1152.7 84.0 reduce-scatter.1
where the time goes:
time: 2180 us; the launch traced here: 2170 us
  waiting for transfers between devices  803 us (37%)
  blocking collectives  790 us (36%)
  local copies, waits for them, and re-layouts  322 us (15%)
  matrix products  193 us (9%)
  other arithmetic  46.6 us (2%)
    all_to_all x1, blocking collectives, body(): lax.all_to_all(spectra, 'band', split_axis=0, concat_axis=1, tiled=True)  731 us
    all_to_all x1, waiting for transfers between devices, body(): lax.all_to_all(summed, 'band', split_axis=2, concat_axis=0, tiled=True)  719 us
    dot_general x1, matrix products, complex_product(): jnp.einsum('fqsk,fqpkr->fpsr', left_part, complex_right(rows_part), prefe...  88.8 us
    reduce_scatter x1, waiting for transfers between devices, body(): lax.psum_scatter(block_terms.astype(jnp.bfloat16), 'rcv', scatter_dimensi...  84.2 us
    reduce_scatter x1, local copies, waits for them, and re-layouts, body(): lax.psum_scatter(block_terms.astype(jnp.bfloat16), 'rcv', scatter_dimensi...  80.4 us
    all_to_all x1, local copies, waits for them, and re-layouts, body(): lax.all_to_all(owned_spec, 'rcv', split_axis=2, concat_axis=3, tiled=True)  80.3 us
    dot_general x1, matrix products, body(): jnp.einsum('fpsr,fpt->srt', source_spec, inverse, preferred_element_type=...  77.5 us
    reshape x1, local copies, waits for them, and re-layouts, body(): owned_spec.reshape(channels // 2, 2, owned_spec.shape[1], owned_spec.shap...  60.1 us
  transfers between devices with their start and end apart: 2, of which 2 were waited for; matrix products, arithmetic and copies ran while one was open for 0% of the time, Pallas kernels for 0%

commit v1 on v0

--- a/solution.py
+++ b/solution.py
@@ -3,7 +3,16 @@
 import jax
 import jax.numpy as jnp
 from jax import lax
+from jax.experimental import pallas as pl
+from jax.experimental.pallas import tpu as pltpu
 from jax.sharding import PartitionSpec as P
+
+OWNERS = ("band", "rcv")
+SLAB = 16
+CHUNKS = 2
+LANES = 256
+TILE = 128
+VMEM = 56 * 2**20
 
 
 def tables(length):
@@ -22,6 +31,205 @@
     return (forward, inverse)
 
 
+def lane_tiles(lanes):
+    return [(k, slice(k * TILE, (k + 1) * TILE)) for k in range(lanes // TILE)]
+
+
+def dft_kernel(traces_ref, table_ref, *refs):
+    outs, scratch = refs[:-1], refs[-1]
+    sources = traces_ref.shape[0]
+    channels = table_ref.shape[0]
+    owners, width = outs[0].shape[0], outs[0].shape[1]
+
+    def transform(s, carry):
+        spectrum = lax.dot_general(
+            table_ref[...], traces_ref[s], (((1,), (1,)), ((), ())), preferred_element_type=jnp.float32
+        )
+        window = pl.ds(pl.multiple_of(s * channels, channels), channels)
+        for k, lanes in lane_tiles(spectrum.shape[1]):
+            scratch[k, window, :] = spectrum[:, lanes]
+        return carry
+
+    lax.fori_loop(0, sources, transform, 0, unroll=2)
+
+    def regroup(owner, carry):
+        for j, out in enumerate(outs):
+            for c in range(width):
+                row = owner * (width * len(outs)) + j * width + c
+                for k, lanes in lane_tiles(out.shape[3]):
+                    out[owner, c, :, lanes] = scratch[
+                        k, pl.ds(row, sources, stride=channels), :
+                    ].astype(jnp.bfloat16)
+        return carry
+
+    lax.fori_loop(0, owners, regroup, 0)
+
+
+def dft(traces, table, first, count, owners, chunks):
+    _, receivers, length = traces.shape
+    lanes = min(LANES, receivers)
+    width = length // (owners * chunks)
+    out = jax.ShapeDtypeStruct((owners, width, count * SLAB, receivers), jnp.bfloat16)
+    out_spec = pl.BlockSpec((owners, width, SLAB, lanes), lambda i, j: (0, 0, i, j))
+    return pl.pallas_call(
+        dft_kernel,
+        grid=(count, receivers // lanes),
+        in_specs=[
+            pl.BlockSpec((SLAB, lanes, length), lambda i, j: (i + first, j, 0)),
+            pl.BlockSpec((length, length), lambda i, j: (0, 0)),
+        ],
+        out_specs=[out_spec] * chunks,
+        out_shape=[out] * chunks,
+        scratch_shapes=[pltpu.VMEM((lanes // TILE, SLAB * length, TILE), jnp.float32)],
+        compiler_params=pltpu.CompilerParams(vmem_limit_bytes=VMEM),
+        name="dft",
+    )(traces, table)
+
+
+def square_kernel(bands, halves, factor, slab_ref, rest_ref, slab_out, rest_out, real, imag):
+    rest = rest_ref.shape[2]
+    sources = SLAB + rest
+    receivers = rest_ref.shape[3]
+    for part, whole in enumerate((real, imag)):
+        for b in range(bands):
+            for v in range(halves):
+                columns = slice(v * receivers, (v + 1) * receivers)
+                whole[b * sources : b * sources + SLAB, columns] = slab_ref[b * halves + v, part]
+                whole[b * sources + SLAB : (b + 1) * sources, columns] = rest_ref[b * halves + v, part]
+
+    def rows(b, carry):
+        window = pl.ds(pl.multiple_of(b * sources, sources), sources)
+        left_real, left_imag = real[window, :], imag[window, :]
+        for v in range(halves):
+            columns = slice(v * receivers, (v + 1) * receivers)
+            dot = lambda x, y: jnp.dot(x, y[:, columns], preferred_element_type=jnp.float32)
+            out_real = (dot(left_real, real) - dot(left_imag, imag)) * factor
+            out_imag = (dot(left_real, imag) + dot(left_imag, real)) * factor
+            for part, value in enumerate((out_real, out_imag)):
+                value = value.astype(jnp.bfloat16)
+                slab_out[b * halves + v, part] = value[:SLAB]
+                rest_out[b * halves + v, part] = value[SLAB:]
+        return carry
+
+    lax.fori_loop(0, bands, rows, 0)
+
+
+def square(slab, rest, chunk, bands, halves, factor):
+    owners, width, count, receivers = rest.shape
+    freqs = width // 2
+    stations = bands * (SLAB + count)
+    first = chunk * freqs
+
+    def kernel(*refs):
+        square_kernel(bands, halves, factor, *refs)
+
+    slab_spec = pl.BlockSpec((owners, 2, SLAB, receivers), lambda f: (0, f, 0, 0))
+    rest_spec = pl.BlockSpec((owners, 2, count, receivers), lambda f: (0, f, 0, 0))
+    return pl.pallas_call(
+        kernel,
+        grid=(freqs,),
+        in_specs=[
+            pl.BlockSpec((owners, 2, SLAB, receivers), lambda f: (0, f + first, 0, 0)),
+            rest_spec,
+        ],
+        out_specs=[slab_spec, rest_spec],
+        out_shape=[
+            jax.ShapeDtypeStruct((owners, width, SLAB, receivers), jnp.bfloat16),
+            jax.ShapeDtypeStruct(rest.shape, jnp.bfloat16),
+        ],
+        scratch_shapes=[pltpu.VMEM((stations, stations), jnp.bfloat16)] * 2,
+        compiler_params=pltpu.CompilerParams(vmem_limit_bytes=VMEM),
+        name="square",
+    )(slab, rest)
+
+
+def inverse_kernel(count, *refs):
+    spectra, table_ref = refs[:count], refs[count]
+    out, scratch = refs[-2], refs[-1]
+    owners, width, sources, lanes = spectra[0].shape
+    channels = owners * width
+    for j, part in enumerate(spectra):
+
+        def widen(owner, carry):
+            start = pl.multiple_of((j * owners + owner) * width * sources, width * sources)
+            block = part[owner].reshape(width * sources, lanes).astype(jnp.float32)
+            for k, window in lane_tiles(lanes):
+                scratch[k, pl.ds(start, width * sources), :] = block[:, window]
+            return carry
+
+        lax.fori_loop(0, owners, widen, 0)
+
+    def transform(s, carry):
+        total = jnp.concatenate(
+            [scratch[k, pl.ds(s, count * channels, stride=sources), :] for k, _ in lane_tiles(lanes)],
+            axis=1,
+        ).astype(jnp.bfloat16)
+        out[s] = lax.dot_general(
+            total, table_ref[...], (((0,), (0,)), ((), ())), preferred_element_type=jnp.float32
+        ).astype(jnp.bfloat16)
+        return carry
+
+    lax.fori_loop(0, sources, transform, 0)
+
+
+def inverse_transform(spectra, table, first, shape, previous):
+    owners, width, rows, receivers = spectra[0].shape
+    length = shape[2]
+    lanes = min(LANES, receivers)
+    count = len(spectra)
+    spec = pl.BlockSpec((owners, width, SLAB, lanes), lambda i, j: (0, 0, i, j))
+    ordered = table.reshape(owners, count, width, length).transpose(1, 0, 2, 3).reshape(length, length)
+
+    def kernel(*refs):
+        inverse_kernel(count, *refs)
+
+    in_specs = [spec] * count + [pl.BlockSpec((length, length), lambda i, j: (0, 0))]
+    operands = list(spectra) + [ordered]
+    aliases = {}
+    if previous is not None:
+        in_specs.append(pl.BlockSpec(memory_space=pl.ANY))
+        operands.append(previous)
+        aliases = {count + 1: 0}
+    return pl.pallas_call(
+        kernel,
+        grid=(rows // SLAB, receivers // lanes),
+        in_specs=in_specs,
+        out_specs=pl.BlockSpec((SLAB, lanes, length), lambda i, j: (i + first, j, 0)),
+        out_shape=jax.ShapeDtypeStruct(shape, jnp.bfloat16),
+        scratch_shapes=[pltpu.VMEM((lanes // TILE, SLAB * length, TILE), jnp.float32)],
+        input_output_aliases=aliases,
+        compiler_params=pltpu.CompilerParams(vmem_limit_bytes=VMEM),
+        name="inverse",
+    )(*operands)
+
+
+def exchange(array):
+    return lax.all_to_all(array, OWNERS, 0, 0)
+
+
+def body(traces):
+    sources, _, length = traces.shape
+    bands, halves = lax.axis_size("band"), lax.axis_size("rcv")
+    owners = bands * halves
+    factor = 1.0 / math.sqrt(sources * bands)
+    forward, inverse = tables(length)
+    inverse = inverse.reshape(length, length)
+    table = forward.T
+    slabs = sources // SLAB - 1
+    (slab,) = dft(traces, table, 0, 1, owners, 1)
+    slab = exchange(slab)
+    rest = dft(traces, table, 1, slabs, owners, CHUNKS)
+    rest = [exchange(part) for part in rest]
+    slab_parts, rest_parts = [], []
+    for chunk in range(CHUNKS):
+        slab_part, rest_part = square(slab, rest[chunk], chunk, bands, halves, factor)
+        slab_parts.append(slab_part)
+        rest_parts.append(exchange(rest_part))
+    last = exchange(jnp.concatenate(slab_parts, axis=1))
+    result = inverse_transform(rest_parts, inverse, 1, traces.shape, None)
+    return inverse_transform([last], inverse, 0, traces.shape, result)
+
+
 def complex_right(rows_part):
     real_part = rows_part[:, 0]
     imag_part = rows_part[:, 1]
@@ -36,7 +244,7 @@
     )
 
 
-def body(traces):
+def general_body(traces):
     length = traces.shape[2]
     stations = traces.shape[0] * lax.axis_size("band")
     factor = jnp.float32(1.0 / math.sqrt(stations))
@@ -57,8 +265,16 @@
     return result.astype(jnp.bfloat16)
 
 
+def choose(traces):
+    sources, _, length = traces.shape
+    owners = lax.axis_size("band") * lax.axis_size("rcv")
+    if sources % SLAB == 0 and sources > SLAB and (length // 2) % (owners * CHUNKS) == 0:
+        return body(traces)
+    return general_body(traces)
+
+
 def solution(mesh):
     placed = (P(("grp", "band"), "rcv", None),)
     return jax.shard_map(
-        body, mesh=mesh, in_specs=placed, out_specs=P(("grp", "band"), "rcv", None), check_vma=False
-    )
+        choose, mesh=mesh, in_specs=placed, out_specs=P(("grp", "band"), "rcv", None), check_vma=False
+    )

time: 2180 us -> 1510 us (0.69)
  blocking collectives: 790 us -> 322 us
  local copies, waits for them, and re-layouts: 322 us -> 2.4 us
  Pallas kernels: 0 us -> 272 us
  matrix products: 193 us -> 0 us
  waiting for transfers between devices: 803 us -> 885 us
  other arithmetic: 46.6 us -> 5.04 us
    all_to_all x2 -> x1, blocking collectives: 790 us -> 322 us  [exchange(): return lax.all_to_all(array, OWNERS, 0, 0)]
    pallas_call x0 -> x6, Pallas kernels: none -> 272 us  [the longest x2 98.7 us: inverse_transform(): pl.pallas_call(kernel, grid=(rows // SLAB, receivers // lanes), in_specs=...]
    dot_general x3 -> x0, matrix products: 193 us -> none  [the longest x1 88.8 us: complex_product(): jnp.einsum('fqsk,fqpkr->fpsr', left_part, complex_right(rows_part), prefe...]
    all_to_all x1 -> x5, waiting for transfers between devices: 719 us -> 885 us  [exchange(): return lax.all_to_all(array, OWNERS, 0, 0)]
    all_to_all x4 -> x0, local copies, waits for them, and re-layouts: 150 us -> none  [the longest x1 80.3 us: body(): lax.all_to_all(owned_spec, 'rcv', split_axis=2, concat_axis=3, tiled=True)]
    reduce_scatter x1 -> x0, waiting for transfers between devices: 84.2 us -> none  [body(): lax.psum_scatter(block_terms.astype(jnp.bfloat16), 'rcv', scatter_dimensi...]
    reduce_scatter x1 -> x0, local copies, waits for them, and re-layouts: 80.4 us -> none  [body(): lax.psum_scatter(block_terms.astype(jnp.bfloat16), 'rcv', scatter_dimensi...]
    reshape x1 -> x0, local copies, waits for them, and re-layouts: 60.1 us -> none  [body(): owned_spec.reshape(channels // 2, 2, owned_spec.shape[1], owned_spec.shap...]
  transfers between devices with their start and end apart: 2 -> 5, of which waited for: 2 -> 5; matrix products, arithmetic and copies ran while one was open for 0% -> 0% of each run, Pallas kernels for 0% -> 16%
where the time goes in v1:
time: 1510 us
  waiting for transfers between devices  885 us (59%)
  blocking collectives  322 us (21%)
  Pallas kernels  272 us (18%)
  starting transfers between devices  27.4 us (2%)
    all_to_all x5, waiting for transfers between devices, exchange(): return lax.all_to_all(array, OWNERS, 0, 0)  885 us
    all_to_all x1, blocking collectives, exchange(): return lax.all_to_all(array, OWNERS, 0, 0)  322 us
    pallas_call x2, Pallas kernels, inverse_transform(): pl.pallas_call(kernel, grid=(rows // SLAB, receivers // lanes), in_specs=...  98.7 us
    pallas_call x2, Pallas kernels, square(): pl.pallas_call(kernel, grid=(freqs,), in_specs=[pl.BlockSpec((owners, 2,...  92.4 us
    pallas_call x2, Pallas kernels, dft(): pl.pallas_call(dft_kernel, grid=(count, receivers // lanes), in_specs=[pl...  80.9 us
  transfers between devices with their start and end apart: 5, of which 5 were waited for; matrix products, arithmetic and copies ran while one was open for 0% of the time, Pallas kernels for 16%

profile of v1, /device:TPU:11, one launch (start us, length us, event | category | flops | bytes accessed | tf_op | source)
XLA Modules:
  0.0 1514.3 jit_solution(3434889533520344897)
XLA Ops:
  0.0 0.5 negate_convert_fusion
  0.6 0.1 copy.6
  0.7 0.7 convert_element_type.49
  1.4 12.3 dft.2
  13.7 6.6 all-to-all-start
  20.3 68.6 %dft.3 = (bf16[16,8,112,512]{3,2,1,0:T(8,128)(2,1)}, bf16[16,8,112,512]{3,2,1,0:T(8,128)(2,1)}) custom-call(bf16[128,512,256]{2,1,0:T(8,128)(2,1)} %traces_ref.3, bf16[256,256]{1,0:T(8,128)(2,1)} %bitcast.6), custom_call_target="tpu_custom_call" | custom-call | tf_op jit(solution)/shard_map/dft/pallas_call | solution.py:74
  88.9 23.9 %all-to-all-done.refs_0_ = bf16[16,16,16,512]{3,2,1,0:T(8,128)(2,1)} async-done(((bf16[16,16,16,512]{3,2,1,0:T(8,128)(2,1)}), bf16[16,16,16,512]{3,2,1,0:T(8,128)(2,1)}, u32[]{:S(2)}, u32[]{:S(2)}) %all-to-all-start) | async-done | bytes 4194336 | tf_op jit(solution)/shard_map/all_to_all | solution.py:207
  112.8 322.4 %all_to_all.30.refs_1_ = bf16[16,8,112,512]{3,2,1,0:T(8,128)(2,1)} all-to-all(bf16[16,8,112,512]{3,2,1,0:T(8,128)(2,1)} %get-tuple-element.13), channel_id=1, replica_groups=mesh['grp'=2,'band'=8,'rcv'=2] {'band','rcv'}, dimensions={0} | all-to-all | bytes 29360128 | tf_op jit(solution)/shard_map/all_to_all | solution.py:207
  435.1 5.9 all-to-all-start.1
  441.0 46.2 %square.3 = (bf16[16,8,16,512]{3,2,1,0:T(8,128)(2,1)}, bf16[16,8,112,512]{3,2,1,0:T(8,128)(2,1)}) custom-call(bf16[16,16,16,512]{3,2,1,0:T(8,128)(2,1)} %all-to-all-done.refs_0_, bf16[16,8,112,512]{3,2,1,0:T(8,128)(2,1)} %all_to_all.30.refs_1_), custom_call_target="tpu_custom_call" | custom-call | tf_op jit(solution)/shard_map/square/pallas_call | solution.py:128
  487.2 271.0 %all-to-all-done.1.refs_1_ = bf16[16,8,112,512]{3,2,1,0:T(8,128)(2,1)} async-done(((bf16[16,8,112,512]{3,2,1,0:T(8,128)(2,1)}), bf16[16,8,112,512]{3,2,1,0:T(8,128)(2,1)}, u32[]{:S(2)}, u32[]{:S(2)}) %all-to-all-start.1) | async-done | bytes 14680096 | tf_op jit(solution)/shard_map/all_to_all | solution.py:207
  758.2 4.9 all-to-all-start.5
  763.2 46.2 %square.2 = (bf16[16,8,16,512]{3,2,1,0:T(8,128)(2,1)}, bf16[16,8,112,512]{3,2,1,0:T(8,128)(2,1)}) custom-call(bf16[16,16,16,512]{3,2,1,0:T(8,128)(2,1)} %all-to-all-done.refs_0_, bf16[16,8,112,512]{3,2,1,0:T(8,128)(2,1)} %all-to-all-done.1.refs_1_), custom_call_target="tpu_custom_call" | custom-call | tf_op jit(solution)/shard_map/square/pallas_call | solution.py:128
  809.4 270.9 %all-to-all-done.5.refs_1_ = bf16[16,8,112,512]{3,2,1,0:T(8,128)(2,1)} async-done(((bf16[16,8,112,512]{3,2,1,0:T(8,128)(2,1)}), bf16[16,8,112,512]{3,2,1,0:T(8,128)(2,1)}, u32[]{:S(2)}, u32[]{:S(2)}) %all-to-all-start.5) | async-done | bytes 14680096 | tf_op jit(solution)/shard_map/all_to_all | solution.py:207
  1080.3 0.0 copy-start
  1080.3 5.1 all-to-all-start.4
  1085.4 0.0 copy-done
  1085.4 3.9 pad_maximum_fusion
  1089.3 313.2 %all-to-all-done.4.refs_0_ = bf16[16,8,112,512]{3,2,1,0:T(8,128)(2,1)} async-done(((bf16[16,8,112,512]{3,2,1,0:T(8,128)(2,1)}), bf16[16,8,112,512]{3,2,1,0:T(8,128)(2,1)}, u32[]{:S(2)}, u32[]{:S(2)}) %all-to-all-start.4) | async-done | bytes 14680096 | tf_op jit(solution)/shard_map/all_to_all | solution.py:207
  1402.5 4.9 all-to-all-start.3
  1407.4 0.6 negate_multiply_fusion
  1408.0 0.1 copy.7
  1408.2 0.1 convert_element_type.53
  1408.3 0.7 convert_element_type.52.refs_1_
  1408.9 0.7 copy.9
  1409.6 84.3 %inverse.2.refs_2_ = bf16[128,512,256]{2,1,0:T(8,128)(2,1)} custom-call(bf16[16,8,112,512]{3,2,1,0:T(8,128)(2,1)} %all-to-all-done.4.refs_0_, bf16[16,8,112,512]{3,2,1,0:T(8,128)(2,1)} %all-to-all-done.5.refs_1_, bf16[256,256]{1,0:T(8,128)(2,1)} %bitcast.7), custom_call_target="tpu_custom_call" | custom-call | tf_op jit(solution)/shard_map/inverse/pallas_call | solution.py:193
  1493.9 6.0 all-to-all-done.3.refs_0_
  1499.9 14.4 inverse.3
  (4 shorter events, 0.0 us)
Async XLA Ops:
  13.7 99.0 %all-to-all-start = ((bf16[16,16,16,512]{3,2,1,0:T(8,128)(2,1)}), bf16[16,16,16,512]{3,2,1,0:T(8,128)(2,1)}, u32[]{:S(2)}, u32[]{:S(2)}) async-start(bf16[16,16,16,512]{3,2,1,0:T(8,128)(2,1)} %dft.2), calls=%async_computation | async-start | bytes 8388608 | tf_op jit(solution)/shard_map/all_to_all | solution.py:207
  435.1 323.1 %all-to-all-start.1 = ((bf16[16,8,112,512]{3,2,1,0:T(8,128)(2,1)}), bf16[16,8,112,512]{3,2,1,0:T(8,128)(2,1)}, u32[]{:S(2)}, u32[]{:S(2)}) async-start(bf16[16,8,112,512]{3,2,1,0:T(8,128)(2,1)} %get-tuple-element.11), calls=%async_computation.1 | async-start | bytes 29360128 | tf_op jit(solution)/shard_map/all_to_all | solution.py:207
  758.2 322.1 %all-to-all-start.5 = ((bf16[16,8,112,512]{3,2,1,0:T(8,128)(2,1)}), bf16[16,8,112,512]{3,2,1,0:T(8,128)(2,1)}, u32[]{:S(2)}, u32[]{:S(2)}) async-start(bf16[16,8,112,512]{3,2,1,0:T(8,128)(2,1)} %get-tuple-element.16), calls=%async_computation.5 | async-start | bytes 29360128 | tf_op jit(solution)/shard_map/all_to_all | solution.py:207
  1080.3 5.1 copy-start
  1080.3 322.2 %all-to-all-start.4 = ((bf16[16,8,112,512]{3,2,1,0:T(8,128)(2,1)}), bf16[16,8,112,512]{3,2,1,0:T(8,128)(2,1)}, u32[]{:S(2)}, u32[]{:S(2)}) async-start(bf16[16,8,112,512]{3,2,1,0:T(8,128)(2,1)} %get-tuple-element.15), calls=%async_computation.4 | async-start | bytes 29360128 | tf_op jit(solution)/shard_map/all_to_all | solution.py:207
  1402.5 97.4 %all-to-all-start.3 = ((bf16[16,16,16,512]{3,2,1,0:T(8,128)(2,1)}), bf16[16,16,16,512]{3,2,1,0:T(8,128)(2,1)}, u32[]{:S(2)}, u32[]{:S(2)}) async-start(bf16[16,16,16,512]{3,2,1,0:T(8,128)(2,1)} %pad_maximum_fusion), calls=%async_computation.3 | async-start | bytes 8388608 | tf_op jit(solution)/shard_map/all_to_all | solution.py:207

commit v2 on v1

--- a/solution.py
+++ b/solution.py
@@ -12,6 +12,7 @@
 CHUNKS = 2
 LANES = 256
 TILE = 128
+PAD = 8
 VMEM = 56 * 2**20
 
 
@@ -45,24 +46,21 @@
         spectrum = lax.dot_general(
             table_ref[...], traces_ref[s], (((1,), (1,)), ((), ())), preferred_element_type=jnp.float32
         )
-        window = pl.ds(pl.multiple_of(s * channels, channels), channels)
         for k, lanes in lane_tiles(spectrum.shape[1]):
-            scratch[k, window, :] = spectrum[:, lanes]
-        return carry
-
-    lax.fori_loop(0, sources, transform, 0, unroll=2)
+            scratch[k, pl.ds(s, channels, stride=sources + PAD), :] = spectrum[:, lanes]
+        return carry
+
+    lax.fori_loop(0, sources, transform, 0, unroll=sources)
 
     def regroup(owner, carry):
         for j, out in enumerate(outs):
             for c in range(width):
-                row = owner * (width * len(outs)) + j * width + c
+                row = (owner * (width * len(outs)) + j * width + c) * (sources + PAD)
                 for k, lanes in lane_tiles(out.shape[3]):
-                    out[owner, c, :, lanes] = scratch[
-                        k, pl.ds(row, sources, stride=channels), :
-                    ].astype(jnp.bfloat16)
-        return carry
-
-    lax.fori_loop(0, owners, regroup, 0)
+                    out[owner, c, :, lanes] = scratch[k, pl.ds(row, sources), :].astype(jnp.bfloat16)
+        return carry
+
+    lax.fori_loop(0, owners, regroup, 0, unroll=4)
 
 
 def dft(traces, table, first, count, owners, chunks):
@@ -80,7 +78,7 @@
         ],
         out_specs=[out_spec] * chunks,
         out_shape=[out] * chunks,
-        scratch_shapes=[pltpu.VMEM((lanes // TILE, SLAB * length, TILE), jnp.float32)],
+        scratch_shapes=[pltpu.VMEM((lanes // TILE, length * (SLAB + PAD), TILE), jnp.float32)],
         compiler_params=pltpu.CompilerParams(vmem_limit_bytes=VMEM),
         name="dft",
     )(traces, table)
@@ -151,17 +149,21 @@
     for j, part in enumerate(spectra):
 
         def widen(owner, carry):
-            start = pl.multiple_of((j * owners + owner) * width * sources, width * sources)
-            block = part[owner].reshape(width * sources, lanes).astype(jnp.float32)
-            for k, window in lane_tiles(lanes):
-                scratch[k, pl.ds(start, width * sources), :] = block[:, window]
+            for c in range(width):
+                row = ((j * owners + owner) * width + c) * (sources + PAD)
+                block = part[owner, c].astype(jnp.float32)
+                for k, window in lane_tiles(lanes):
+                    scratch[k, pl.ds(row, sources), :] = block[:, window]
             return carry
 
-        lax.fori_loop(0, owners, widen, 0)
+        lax.fori_loop(0, owners, widen, 0, unroll=2)
 
     def transform(s, carry):
         total = jnp.concatenate(
-            [scratch[k, pl.ds(s, count * channels, stride=sources), :] for k, _ in lane_tiles(lanes)],
+            [
+                scratch[k, pl.ds(s, count * channels, stride=sources + PAD), :]
+                for k, _ in lane_tiles(lanes)
+            ],
             axis=1,
         ).astype(jnp.bfloat16)
         out[s] = lax.dot_general(
@@ -169,7 +171,7 @@
         ).astype(jnp.bfloat16)
         return carry
 
-    lax.fori_loop(0, sources, transform, 0)
+    lax.fori_loop(0, sources, transform, 0, unroll=8)
 
 
 def inverse_transform(spectra, table, first, shape, previous):
@@ -196,7 +198,7 @@
         in_specs=in_specs,
         out_specs=pl.BlockSpec((SLAB, lanes, length), lambda i, j: (i + first, j, 0)),
         out_shape=jax.ShapeDtypeStruct(shape, jnp.bfloat16),
-        scratch_shapes=[pltpu.VMEM((lanes // TILE, SLAB * length, TILE), jnp.float32)],
+        scratch_shapes=[pltpu.VMEM((lanes // TILE, length * (SLAB + PAD), TILE), jnp.float32)],
         input_output_aliases=aliases,
         compiler_params=pltpu.CompilerParams(vmem_limit_bytes=VMEM),
         name="inverse",

time: 1510 us -> 1500 us (level)
  Pallas kernels: 272 us -> 162 us
  waiting for transfers between devices: 885 us -> 980 us
    all_to_all x5, waiting for transfers between devices: 885 us -> 980 us  [exchange(): return lax.all_to_all(array, OWNERS, 0, 0)]
    pallas_call x2, Pallas kernels: 98.7 us -> 35.1 us  [inverse_transform(): pl.pallas_call(kernel, grid=(rows // SLAB, receivers // lanes), in_specs=...]
    pallas_call x2, Pallas kernels: 80.9 us -> 34.4 us  [dft(): pl.pallas_call(dft_kernel, grid=(count, receivers // lanes), in_specs=[pl...]
  transfers between devices with their start and end apart: 5 -> 5, of which waited for: 5 -> 5; matrix products, arithmetic and copies ran while one was open for 0% -> 0% of each run, Pallas kernels for 16% -> 10%
where the time goes in v2:
time: 1500 us
  waiting for transfers between devices  980 us (65%)
  blocking collectives  322 us (21%)
  Pallas kernels  162 us (11%)
  starting transfers between devices  27.4 us (2%)
    all_to_all x5, waiting for transfers between devices, exchange(): return lax.all_to_all(array, OWNERS, 0, 0)  980 us
    all_to_all x1, blocking collectives, exchange(): return lax.all_to_all(array, OWNERS, 0, 0)  322 us
    pallas_call x2, Pallas kernels, square(): pl.pallas_call(kernel, grid=(freqs,), in_specs=[pl.BlockSpec((owners, 2,...  92.4 us
    pallas_call x2, Pallas kernels, inverse_transform(): pl.pallas_call(kernel, grid=(rows // SLAB, receivers // lanes), in_specs=...  35.1 us
    pallas_call x2, Pallas kernels, dft(): pl.pallas_call(dft_kernel, grid=(count, receivers // lanes), in_specs=[pl...  34.4 us
  transfers between devices with their start and end apart: 5, of which 5 were waited for; matrix products, arithmetic and copies ran while one was open for 0% of the time, Pallas kernels for 10%

profile of v2, /device:TPU:11, one launch (start us, length us, event | category | flops | bytes accessed | tf_op | source)
XLA Modules:
  0.0 1498.7 jit_solution(63063457105621999)
XLA Ops:
  0.0 0.5 negate_convert_fusion
  0.6 0.1 copy.6
  0.7 0.7 convert_element_type.49
  1.4 5.4 dft.2
  6.8 6.6 all-to-all-start
  13.4 29.0 %dft.3 = (bf16[16,8,112,512]{3,2,1,0:T(8,128)(2,1)}, bf16[16,8,112,512]{3,2,1,0:T(8,128)(2,1)}) custom-call(bf16[128,512,256]{2,1,0:T(8,128)(2,1)} %traces_ref.3, bf16[256,256]{1,0:T(8,128)(2,1)} %bitcast.6), custom_call_target="tpu_custom_call" | custom-call | tf_op jit(solution)/shard_map/dft/pallas_call | solution.py:72
  42.4 63.5 %all-to-all-done.refs_0_ = bf16[16,16,16,512]{3,2,1,0:T(8,128)(2,1)} async-done(((bf16[16,16,16,512]{3,2,1,0:T(8,128)(2,1)}), bf16[16,16,16,512]{3,2,1,0:T(8,128)(2,1)}, u32[]{:S(2)}, u32[]{:S(2)}) %all-to-all-start) | async-done | bytes 4194336 | tf_op jit(solution)/shard_map/all_to_all | solution.py:209
  105.9 322.4 %all_to_all.30.refs_1_ = bf16[16,8,112,512]{3,2,1,0:T(8,128)(2,1)} all-to-all(bf16[16,8,112,512]{3,2,1,0:T(8,128)(2,1)} %get-tuple-element.13), channel_id=1, replica_groups=mesh['grp'=2,'band'=8,'rcv'=2] {'band','rcv'}, dimensions={0} | all-to-all | bytes 29360128 | tf_op jit(solution)/shard_map/all_to_all | solution.py:209
  428.2 5.9 all-to-all-start.1
  434.1 46.2 %square.3 = (bf16[16,8,16,512]{3,2,1,0:T(8,128)(2,1)}, bf16[16,8,112,512]{3,2,1,0:T(8,128)(2,1)}) custom-call(bf16[16,16,16,512]{3,2,1,0:T(8,128)(2,1)} %all-to-all-done.refs_0_, bf16[16,8,112,512]{3,2,1,0:T(8,128)(2,1)} %all_to_all.30.refs_1_), custom_call_target="tpu_custom_call" | custom-call | tf_op jit(solution)/shard_map/square/pallas_call | solution.py:126
  480.3 271.0 %all-to-all-done.1.refs_1_ = bf16[16,8,112,512]{3,2,1,0:T(8,128)(2,1)} async-done(((bf16[16,8,112,512]{3,2,1,0:T(8,128)(2,1)}), bf16[16,8,112,512]{3,2,1,0:T(8,128)(2,1)}, u32[]{:S(2)}, u32[]{:S(2)}) %all-to-all-start.1) | async-done | bytes 14680096 | tf_op jit(solution)/shard_map/all_to_all | solution.py:209
  751.3 4.9 all-to-all-start.5
  756.3 46.2 %square.2 = (bf16[16,8,16,512]{3,2,1,0:T(8,128)(2,1)}, bf16[16,8,112,512]{3,2,1,0:T(8,128)(2,1)}) custom-call(bf16[16,16,16,512]{3,2,1,0:T(8,128)(2,1)} %all-to-all-done.refs_0_, bf16[16,8,112,512]{3,2,1,0:T(8,128)(2,1)} %all-to-all-done.1.refs_1_), custom_call_target="tpu_custom_call" | custom-call | tf_op jit(solution)/shard_map/square/pallas_call | solution.py:126
  802.4 271.0 %all-to-all-done.5.refs_1_ = bf16[16,8,112,512]{3,2,1,0:T(8,128)(2,1)} async-done(((bf16[16,8,112,512]{3,2,1,0:T(8,128)(2,1)}), bf16[16,8,112,512]{3,2,1,0:T(8,128)(2,1)}, u32[]{:S(2)}, u32[]{:S(2)}) %all-to-all-start.5) | async-done | bytes 14680096 | tf_op jit(solution)/shard_map/all_to_all | solution.py:209
  1073.4 0.0 copy-start
  1073.4 5.1 all-to-all-start.4
  1078.5 0.0 copy-done
  1078.5 3.9 pad_maximum_fusion
  1082.4 313.2 %all-to-all-done.4.refs_0_ = bf16[16,8,112,512]{3,2,1,0:T(8,128)(2,1)} async-done(((bf16[16,8,112,512]{3,2,1,0:T(8,128)(2,1)}), bf16[16,8,112,512]{3,2,1,0:T(8,128)(2,1)}, u32[]{:S(2)}, u32[]{:S(2)}) %all-to-all-start.4) | async-done | bytes 14680096 | tf_op jit(solution)/shard_map/all_to_all | solution.py:209
  1395.6 4.9 all-to-all-start.3
  1400.5 0.6 negate_multiply_fusion
  1401.1 0.1 copy.7
  1401.3 0.1 convert_element_type.53
  1401.3 0.7 convert_element_type.52.refs_1_
  1402.0 0.7 copy.9
  1402.7 29.3 %inverse.2.refs_2_ = bf16[128,512,256]{2,1,0:T(8,128)(2,1)} custom-call(bf16[16,8,112,512]{3,2,1,0:T(8,128)(2,1)} %all-to-all-done.4.refs_0_, bf16[16,8,112,512]{3,2,1,0:T(8,128)(2,1)} %all-to-all-done.5.refs_1_, bf16[256,256]{1,0:T(8,128)(2,1)} %bitcast.7), custom_call_target="tpu_custom_call" | custom-call | tf_op jit(solution)/shard_map/inverse/pallas_call | solution.py:195
  1432.0 61.0 %all-to-all-done.3.refs_0_ = bf16[16,16,16,512]{3,2,1,0:T(8,128)(2,1)} async-done(((bf16[16,16,16,512]{3,2,1,0:T(8,128)(2,1)}), bf16[16,16,16,512]{3,2,1,0:T(8,128)(2,1)}, u32[]{:S(2)}, u32[]{:S(2)}) %all-to-all-start.3) | async-done | bytes 4194336 | tf_op jit(solution)/shard_map/all_to_all | solution.py:209
  1493.0 5.7 inverse.3
  (4 shorter events, 0.0 us)
Async XLA Ops:
  6.8 99.0 %all-to-all-start = ((bf16[16,16,16,512]{3,2,1,0:T(8,128)(2,1)}), bf16[16,16,16,512]{3,2,1,0:T(8,128)(2,1)}, u32[]{:S(2)}, u32[]{:S(2)}) async-start(bf16[16,16,16,512]{3,2,1,0:T(8,128)(2,1)} %dft.2), calls=%async_computation | async-start | bytes 8388608 | tf_op jit(solution)/shard_map/all_to_all | solution.py:209
  428.2 323.1 %all-to-all-start.1 = ((bf16[16,8,112,512]{3,2,1,0:T(8,128)(2,1)}), bf16[16,8,112,512]{3,2,1,0:T(8,128)(2,1)}, u32[]{:S(2)}, u32[]{:S(2)}) async-start(bf16[16,8,112,512]{3,2,1,0:T(8,128)(2,1)} %get-tuple-element.11), calls=%async_computation.1 | async-start | bytes 29360128 | tf_op jit(solution)/shard_map/all_to_all | solution.py:209
  751.3 322.1 %all-to-all-start.5 = ((bf16[16,8,112,512]{3,2,1,0:T(8,128)(2,1)}), bf16[16,8,112,512]{3,2,1,0:T(8,128)(2,1)}, u32[]{:S(2)}, u32[]{:S(2)}) async-start(bf16[16,8,112,512]{3,2,1,0:T(8,128)(2,1)} %get-tuple-element.16), calls=%async_computation.5 | async-start | bytes 29360128 | tf_op jit(solution)/shard_map/all_to_all | solution.py:209
  1073.4 5.1 copy-start
  1073.4 322.2 %all-to-all-start.4 = ((bf16[16,8,112,512]{3,2,1,0:T(8,128)(2,1)}), bf16[16,8,112,512]{3,2,1,0:T(8,128)(2,1)}, u32[]{:S(2)}, u32[]{:S(2)}) async-start(bf16[16,8,112,512]{3,2,1,0:T(8,128)(2,1)} %get-tuple-element.15), calls=%async_computation.4 | async-start | bytes 29360128 | tf_op jit(solution)/shard_map/all_to_all | solution.py:209
  1395.6 97.4 %all-to-all-start.3 = ((bf16[16,16,16,512]{3,2,1,0:T(8,128)(2,1)}), bf16[16,16,16,512]{3,2,1,0:T(8,128)(2,1)}, u32[]{:S(2)}, u32[]{:S(2)}) async-start(bf16[16,16,16,512]{3,2,1,0:T(8,128)(2,1)} %pad_maximum_fusion), calls=%async_computation.3 | async-start | bytes 8388608 | tf_op jit(solution)/shard_map/all_to_all | solution.py:209

commit v3 on v2

--- a/solution.py
+++ b/solution.py
@@ -2,17 +2,18 @@
 
 import jax
 import jax.numpy as jnp
+import numpy as np
 from jax import lax
 from jax.experimental import pallas as pl
 from jax.experimental.pallas import tpu as pltpu
 from jax.sharding import PartitionSpec as P
 
 OWNERS = ("band", "rcv")
-SLAB = 16
+SLAB = 8
+BLOCK = 24
 CHUNKS = 2
 LANES = 256
 TILE = 128
-PAD = 8
 VMEM = 56 * 2**20
 
 
@@ -32,6 +33,16 @@
     return (forward, inverse)
 
 
+def constant_tables(length):
+    phase = np.arange(length // 2)[:, None] * np.arange(length)[None, :] % length
+    angles = phase.astype(np.float32) * np.float32(2.0 * math.pi / length)
+    factor = np.float32(1.0 / math.sqrt(length))
+    forward = np.stack([np.cos(angles) * factor, -(np.sin(angles) * factor)], axis=1)
+    weights = np.where(np.arange(length // 2) == 0, 1.0, 2.0).astype(np.float32)
+    inverse = forward * weights[:, None, None]
+    return [array.reshape(length, length).astype(jnp.bfloat16) for array in (forward, inverse)]
+
+
 def lane_tiles(lanes):
     return [(k, slice(k * TILE, (k + 1) * TILE)) for k in range(lanes // TILE)]
 
@@ -47,15 +58,15 @@
             table_ref[...], traces_ref[s], (((1,), (1,)), ((), ())), preferred_element_type=jnp.float32
         )
         for k, lanes in lane_tiles(spectrum.shape[1]):
-            scratch[k, pl.ds(s, channels, stride=sources + PAD), :] = spectrum[:, lanes]
-        return carry
-
-    lax.fori_loop(0, sources, transform, 0, unroll=sources)
+            scratch[k, pl.ds(s, channels, stride=sources), :] = spectrum[:, lanes]
+        return carry
+
+    lax.fori_loop(0, sources, transform, 0, unroll=8)
 
     def regroup(owner, carry):
         for j, out in enumerate(outs):
             for c in range(width):
-                row = (owner * (width * len(outs)) + j * width + c) * (sources + PAD)
+                row = (owner * (width * len(outs)) + j * width + c) * sources
                 for k, lanes in lane_tiles(out.shape[3]):
                     out[owner, c, :, lanes] = scratch[k, pl.ds(row, sources), :].astype(jnp.bfloat16)
         return carry
@@ -63,22 +74,22 @@
     lax.fori_loop(0, owners, regroup, 0, unroll=4)
 
 
-def dft(traces, table, first, count, owners, chunks):
+def dft(traces, table, first, count, rows, owners, chunks):
     _, receivers, length = traces.shape
     lanes = min(LANES, receivers)
     width = length // (owners * chunks)
-    out = jax.ShapeDtypeStruct((owners, width, count * SLAB, receivers), jnp.bfloat16)
-    out_spec = pl.BlockSpec((owners, width, SLAB, lanes), lambda i, j: (0, 0, i, j))
+    out = jax.ShapeDtypeStruct((owners, width, count * rows, receivers), jnp.bfloat16)
+    out_spec = pl.BlockSpec((owners, width, rows, lanes), lambda i, j: (0, 0, i, j))
     return pl.pallas_call(
         dft_kernel,
         grid=(count, receivers // lanes),
         in_specs=[
-            pl.BlockSpec((SLAB, lanes, length), lambda i, j: (i + first, j, 0)),
+            pl.BlockSpec((rows, lanes, length), lambda i, j: (i + first, j, 0)),
             pl.BlockSpec((length, length), lambda i, j: (0, 0)),
         ],
         out_specs=[out_spec] * chunks,
         out_shape=[out] * chunks,
-        scratch_shapes=[pltpu.VMEM((lanes // TILE, length * (SLAB + PAD), TILE), jnp.float32)],
+        scratch_shapes=[pltpu.VMEM((lanes // TILE, length * rows, TILE), jnp.float32)],
         compiler_params=pltpu.CompilerParams(vmem_limit_bytes=VMEM),
         name="dft",
     )(traces, table)
@@ -92,8 +103,8 @@
         for b in range(bands):
             for v in range(halves):
                 columns = slice(v * receivers, (v + 1) * receivers)
-                whole[b * sources : b * sources + SLAB, columns] = slab_ref[b * halves + v, part]
-                whole[b * sources + SLAB : (b + 1) * sources, columns] = rest_ref[b * halves + v, part]
+                whole[b * sources : b * sources + rest, columns] = rest_ref[b * halves + v, part]
+                whole[b * sources + rest : (b + 1) * sources, columns] = slab_ref[b * halves + v, part]
 
     def rows(b, carry):
         window = pl.ds(pl.multiple_of(b * sources, sources), sources)
@@ -105,8 +116,8 @@
             out_imag = (dot(left_real, imag) + dot(left_imag, real)) * factor
             for part, value in enumerate((out_real, out_imag)):
                 value = value.astype(jnp.bfloat16)
-                slab_out[b * halves + v, part] = value[:SLAB]
-                rest_out[b * halves + v, part] = value[SLAB:]
+                rest_out[b * halves + v, part] = value[:rest]
+                slab_out[b * halves + v, part] = value[rest:]
         return carry
 
     lax.fori_loop(0, bands, rows, 0)
@@ -150,7 +161,7 @@
 
         def widen(owner, carry):
             for c in range(width):
-                row = ((j * owners + owner) * width + c) * (sources + PAD)
+                row = ((j * owners + owner) * width + c) * sources
                 block = part[owner, c].astype(jnp.float32)
                 for k, window in lane_tiles(lanes):
                     scratch[k, pl.ds(row, sources), :] = block[:, window]
@@ -161,7 +172,7 @@
     def transform(s, carry):
         total = jnp.concatenate(
             [
-                scratch[k, pl.ds(s, count * channels, stride=sources + PAD), :]
+                scratch[k, pl.ds(s, count * channels, stride=sources), :]
                 for k, _ in lane_tiles(lanes)
             ],
             axis=1,
@@ -174,12 +185,12 @@
     lax.fori_loop(0, sources, transform, 0, unroll=8)
 
 
-def inverse_transform(spectra, table, first, shape, previous):
-    owners, width, rows, receivers = spectra[0].shape
+def inverse_transform(spectra, table, first, rows, shape, previous):
+    owners, width, total, receivers = spectra[0].shape
     length = shape[2]
     lanes = min(LANES, receivers)
     count = len(spectra)
-    spec = pl.BlockSpec((owners, width, SLAB, lanes), lambda i, j: (0, 0, i, j))
+    spec = pl.BlockSpec((owners, width, rows, lanes), lambda i, j: (0, 0, i, j))
     ordered = table.reshape(owners, count, width, length).transpose(1, 0, 2, 3).reshape(length, length)
 
     def kernel(*refs):
@@ -194,11 +205,11 @@
         aliases = {count + 1: 0}
     return pl.pallas_call(
         kernel,
-        grid=(rows // SLAB, receivers // lanes),
+        grid=(total // rows, receivers // lanes),
         in_specs=in_specs,
-        out_specs=pl.BlockSpec((SLAB, lanes, length), lambda i, j: (i + first, j, 0)),
+        out_specs=pl.BlockSpec((rows, lanes, length), lambda i, j: (i + first, j, 0)),
         out_shape=jax.ShapeDtypeStruct(shape, jnp.bfloat16),
-        scratch_shapes=[pltpu.VMEM((lanes // TILE, length * (SLAB + PAD), TILE), jnp.float32)],
+        scratch_shapes=[pltpu.VMEM((lanes // TILE, length * rows, TILE), jnp.float32)],
         input_output_aliases=aliases,
         compiler_params=pltpu.CompilerParams(vmem_limit_bytes=VMEM),
         name="inverse",
@@ -214,13 +225,11 @@
     bands, halves = lax.axis_size("band"), lax.axis_size("rcv")
     owners = bands * halves
     factor = 1.0 / math.sqrt(sources * bands)
-    forward, inverse = tables(length)
-    inverse = inverse.reshape(length, length)
-    table = forward.T
-    slabs = sources // SLAB - 1
-    (slab,) = dft(traces, table, 0, 1, owners, 1)
+    table, inverse = constant_tables(length)
+    rest_count = sources - SLAB
+    (slab,) = dft(traces, table, rest_count // SLAB, 1, SLAB, owners, 1)
     slab = exchange(slab)
-    rest = dft(traces, table, 1, slabs, owners, CHUNKS)
+    rest = dft(traces, table, 0, rest_count // BLOCK, BLOCK, owners, CHUNKS)
     rest = [exchange(part) for part in rest]
     slab_parts, rest_parts = [], []
     for chunk in range(CHUNKS):
@@ -228,8 +237,8 @@
         slab_parts.append(slab_part)
         rest_parts.append(exchange(rest_part))
     last = exchange(jnp.concatenate(slab_parts, axis=1))
-    result = inverse_transform(rest_parts, inverse, 1, traces.shape, None)
-    return inverse_transform([last], inverse, 0, traces.shape, result)
+    result = inverse_transform(rest_parts, inverse, 0, BLOCK, traces.shape, None)
+    return inverse_transform([last], inverse, rest_count // SLAB, SLAB, traces.shape, result)
 
 
 def complex_right(rows_part):
@@ -270,7 +279,9 @@
 def choose(traces):
     sources, _, length = traces.shape
     owners = lax.axis_size("band") * lax.axis_size("rcv")
-    if sources % SLAB == 0 and sources > SLAB and (length // 2) % (owners * CHUNKS) == 0:
+    rest = sources - SLAB
+    fits = sources % SLAB == 0 and rest > 0 and rest % BLOCK == 0
+    if fits and (length // 2) % (owners * CHUNKS) == 0:
         return body(traces)
     return general_body(traces)
 

time: 1500 us -> 1500 us (level)
  blocking collectives: 322 us -> 345 us
  waiting for transfers between devices: 980 us -> 962 us
    all_to_all x1, blocking collectives: 322 us -> 345 us  [exchange(): return lax.all_to_all(array, OWNERS, 0, 0)]
    all_to_all x5, waiting for transfers between devices: 980 us -> 962 us  [exchange(): return lax.all_to_all(array, OWNERS, 0, 0)]
where the time goes in v3:
time: 1500 us; the launch traced here: 1490 us
  waiting for transfers between devices  962 us (64%)
  blocking collectives  345 us (23%)
  Pallas kernels  158 us (11%)
  starting transfers between devices  27.6 us (2%)
    all_to_all x5, waiting for transfers between devices, exchange(): return lax.all_to_all(array, OWNERS, 0, 0)  962 us
    all_to_all x1, blocking collectives, exchange(): return lax.all_to_all(array, OWNERS, 0, 0)  345 us
    pallas_call x2, Pallas kernels, square(): pl.pallas_call(kernel, grid=(freqs,), in_specs=[pl.BlockSpec((owners, 2,...  92.3 us
    pallas_call x2, Pallas kernels, inverse_transform(): pl.pallas_call(kernel, grid=(total // rows, receivers // lanes), in_specs...  32.9 us
    pallas_call x2, Pallas kernels, dft(): pl.pallas_call(dft_kernel, grid=(count, receivers // lanes), in_specs=[pl...  32.5 us
  transfers between devices with their start and end apart: 5, of which 5 were waited for; matrix products, arithmetic and copies ran while one was open for 0% of the time, Pallas kernels for 10%

profile of v3, /device:TPU:11, one launch (start us, length us, event | category | flops | bytes accessed | tf_op | source)
XLA Modules:
  0.0 1494.7 jit_solution(4929605914643898211)
XLA Ops:
  0.0 3.6 dft.2
  3.6 6.6 all-to-all-start
  10.2 28.9 %dft.3 = (bf16[16,8,120,512]{3,2,1,0:T(8,128)(2,1)}, bf16[16,8,120,512]{3,2,1,0:T(8,128)(2,1)}) custom-call(bf16[128,512,256]{2,1,0:T(8,128)(2,1)} %traces_ref.3, bf16[256,256]{1,0:T(8,128)(2,1)} %constant.6.clone.table_ref), custom_call_target="tpu_custom_call" | custom-call | tf_op jit(solution)/shard_map/dft/pallas_call | solution.py:83
  39.1 18.5 %all-to-all-done.refs_0_ = bf16[16,16,8,512]{3,2,1,0:T(8,128)(2,1)S(1)} async-done(((bf16[16,16,8,512]{3,2,1,0:T(8,128)(2,1)}), bf16[16,16,8,512]{3,2,1,0:T(8,128)(2,1)S(1)}, u32[]{:S(2)}, u32[]{:S(2)}) %all-to-all-start) | async-done | bytes 2097184 | tf_op jit(solution)/shard_map/all_to_all | solution.py:220
  57.6 0.0 copy-start
  57.6 344.8 %all_to_all.30.refs_1_ = bf16[16,8,120,512]{3,2,1,0:T(8,128)(2,1)} all-to-all(bf16[16,8,120,512]{3,2,1,0:T(8,128)(2,1)} %get-tuple-element.13), channel_id=1, replica_groups=mesh['grp'=2,'band'=8,'rcv'=2] {'band','rcv'}, dimensions={0} | all-to-all | bytes 31457280 | tf_op jit(solution)/shard_map/all_to_all | solution.py:220
  402.4 0.0 copy-done
  402.4 6.1 all-to-all-start.1
  408.5 46.2 %square.3 = (bf16[16,8,8,512]{3,2,1,0:T(8,128)(2,1)}, bf16[16,8,120,512]{3,2,1,0:T(8,128)(2,1)}) custom-call(bf16[16,16,8,512]{3,2,1,0:T(8,128)(2,1)} %copy-done, bf16[16,8,120,512]{3,2,1,0:T(8,128)(2,1)} %all_to_all.30.refs_1_), custom_call_target="tpu_custom_call" | custom-call | tf_op jit(solution)/shard_map/square/pallas_call | solution.py:137
  454.7 293.5 %all-to-all-done.1.refs_1_ = bf16[16,8,120,512]{3,2,1,0:T(8,128)(2,1)} async-done(((bf16[16,8,120,512]{3,2,1,0:T(8,128)(2,1)}), bf16[16,8,120,512]{3,2,1,0:T(8,128)(2,1)}, u32[]{:S(2)}, u32[]{:S(2)}) %all-to-all-start.1) | async-done | bytes 15728672 | tf_op jit(solution)/shard_map/all_to_all | solution.py:220
  748.1 5.0 all-to-all-start.5
  753.1 46.2 %square.2 = (bf16[16,8,8,512]{3,2,1,0:T(8,128)(2,1)}, bf16[16,8,120,512]{3,2,1,0:T(8,128)(2,1)}) custom-call(bf16[16,16,8,512]{3,2,1,0:T(8,128)(2,1)} %copy-done, bf16[16,8,120,512]{3,2,1,0:T(8,128)(2,1)} %all-to-all-done.1.refs_1_), custom_call_target="tpu_custom_call" | custom-call | tf_op jit(solution)/shard_map/square/pallas_call | solution.py:137
  799.3 293.4 %all-to-all-done.5.refs_1_ = bf16[16,8,120,512]{3,2,1,0:T(8,128)(2,1)} async-done(((bf16[16,8,120,512]{3,2,1,0:T(8,128)(2,1)}), bf16[16,8,120,512]{3,2,1,0:T(8,128)(2,1)}, u32[]{:S(2)}, u32[]{:S(2)}) %all-to-all-start.5) | async-done | bytes 15728672 | tf_op jit(solution)/shard_map/all_to_all | solution.py:220
  1092.7 0.0 copy-start.2
  1092.7 0.0 copy-start.3
  1092.7 5.1 all-to-all-start.4
  1097.8 0.0 copy-done.2
  1097.8 0.0 copy-done.3
  1097.8 1.5 pad_maximum_fusion
  1099.3 338.1 %all-to-all-done.4.refs_0_ = bf16[16,8,120,512]{3,2,1,0:T(8,128)(2,1)} async-done(((bf16[16,8,120,512]{3,2,1,0:T(8,128)(2,1)}), bf16[16,8,120,512]{3,2,1,0:T(8,128)(2,1)}, u32[]{:S(2)}, u32[]{:S(2)}) %all-to-all-start.4) | async-done | bytes 15728672 | tf_op jit(solution)/shard_map/all_to_all | solution.py:220
  1437.4 4.9 all-to-all-start.3
  1442.3 29.3 %inverse.2.refs_2_ = bf16[128,512,256]{2,1,0:T(8,128)(2,1)} custom-call(bf16[16,8,120,512]{3,2,1,0:T(8,128)(2,1)} %all-to-all-done.4.refs_0_, bf16[16,8,120,512]{3,2,1,0:T(8,128)(2,1)} %all-to-all-done.5.refs_1_, bf16[256,256]{1,0:T(8,128)(2,1)} %constant.7.clone.refs_2_), custom_call_target="tpu_custom_call" | custom-call | tf_op jit(solution)/shard_map/inverse/pallas_call | solution.py:206
  1471.6 18.1 %all-to-all-done.3.refs_0_ = bf16[16,16,8,512]{3,2,1,0:T(8,128)(2,1)S(1)} async-done(((bf16[16,16,8,512]{3,2,1,0:T(8,128)(2,1)}), bf16[16,16,8,512]{3,2,1,0:T(8,128)(2,1)S(1)}, u32[]{:S(2)}, u32[]{:S(2)}) %all-to-all-start.3) | async-done | bytes 2097184 | tf_op jit(solution)/shard_map/all_to_all | solution.py:220
  1489.7 0.0 copy-start.1
  1489.7 1.3 copy-done.1
  1491.0 3.6 inverse.3
Async XLA Ops:
  3.6 54.0 %all-to-all-start = ((bf16[16,16,8,512]{3,2,1,0:T(8,128)(2,1)}), bf16[16,16,8,512]{3,2,1,0:T(8,128)(2,1)S(1)}, u32[]{:S(2)}, u32[]{:S(2)}) async-start(bf16[16,16,8,512]{3,2,1,0:T(8,128)(2,1)} %dft.2), calls=%async_computation | async-start | bytes 4194304 | tf_op jit(solution)/shard_map/all_to_all | solution.py:220
  57.6 344.8 %copy-start = (bf16[16,16,8,512]{3,2,1,0:T(8,128)(2,1)}, bf16[16,16,8,512]{3,2,1,0:T(8,128)(2,1)S(1)}, u32[]{:S(2)}) copy-start(bf16[16,16,8,512]{3,2,1,0:T(8,128)(2,1)S(1)} %all-to-all-done.refs_0_) | copy-start | bytes 6291460
  402.4 345.7 %all-to-all-start.1 = ((bf16[16,8,120,512]{3,2,1,0:T(8,128)(2,1)}), bf16[16,8,120,512]{3,2,1,0:T(8,128)(2,1)}, u32[]{:S(2)}, u32[]{:S(2)}) async-start(bf16[16,8,120,512]{3,2,1,0:T(8,128)(2,1)} %get-tuple-element.11), calls=%async_computation.1 | async-start | bytes 31457280 | tf_op jit(solution)/shard_map/all_to_all | solution.py:220
  748.1 344.6 %all-to-all-start.5 = ((bf16[16,8,120,512]{3,2,1,0:T(8,128)(2,1)}), bf16[16,8,120,512]{3,2,1,0:T(8,128)(2,1)}, u32[]{:S(2)}, u32[]{:S(2)}) async-start(bf16[16,8,120,512]{3,2,1,0:T(8,128)(2,1)} %get-tuple-element.16), calls=%async_computation.5 | async-start | bytes 31457280 | tf_op jit(solution)/shard_map/all_to_all | solution.py:220
  1092.7 5.1 copy-start.2
  1092.7 5.1 copy-start.3
  1092.7 344.7 %all-to-all-start.4 = ((bf16[16,8,120,512]{3,2,1,0:T(8,128)(2,1)}), bf16[16,8,120,512]{3,2,1,0:T(8,128)(2,1)}, u32[]{:S(2)}, u32[]{:S(2)}) async-start(bf16[16,8,120,512]{3,2,1,0:T(8,128)(2,1)} %get-tuple-element.15), calls=%async_computation.4 | async-start | bytes 31457280 | tf_op jit(solution)/shard_map/all_to_all | solution.py:220
  1437.4 52.3 %all-to-all-start.3 = ((bf16[16,16,8,512]{3,2,1,0:T(8,128)(2,1)}), bf16[16,16,8,512]{3,2,1,0:T(8,128)(2,1)S(1)}, u32[]{:S(2)}, u32[]{:S(2)}) async-start(bf16[16,16,8,512]{3,2,1,0:T(8,128)(2,1)} %pad_maximum_fusion), calls=%async_computation.3 | async-start | bytes 4194304 | tf_op jit(solution)/shard_map/all_to_all | solution.py:220
  1489.7 1.3 copy-start.1

commit v4 on v3

--- a/solution.py
+++ b/solution.py
@@ -14,7 +14,7 @@
 CHUNKS = 2
 LANES = 256
 TILE = 128
-VMEM = 56 * 2**20
+VMEM = 62 * 2**20
 
 
 def tables(length):

time: 1500 us -> 1490 us (level)
  no operation moved by 1% of the time
where the time goes in v4:
time: 1490 us
  waiting for transfers between devices  962 us (65%)
  blocking collectives  345 us (23%)
  Pallas kernels  158 us (11%)
  starting transfers between devices  27.6 us (2%)
    all_to_all x5, waiting for transfers between devices, exchange(): return lax.all_to_all(array, OWNERS, 0, 0)  962 us
    all_to_all x1, blocking collectives, exchange(): return lax.all_to_all(array, OWNERS, 0, 0)  345 us
    pallas_call x2, Pallas kernels, square(): pl.pallas_call(kernel, grid=(freqs,), in_specs=[pl.BlockSpec((owners, 2,...  92.3 us
    pallas_call x2, Pallas kernels, inverse_transform(): pl.pallas_call(kernel, grid=(total // rows, receivers // lanes), in_specs...  32.9 us
    pallas_call x2, Pallas kernels, dft(): pl.pallas_call(dft_kernel, grid=(count, receivers // lanes), in_specs=[pl...  32.5 us
  transfers between devices with their start and end apart: 5, of which 5 were waited for; matrix products, arithmetic and copies ran while one was open for 0% of the time, Pallas kernels for 10%

profile of v4, /device:TPU:11, one launch (start us, length us, event | category | flops | bytes accessed | tf_op | source)
XLA Modules:
  0.0 1493.5 jit_solution(16741970067151091621)
XLA Ops:
  0.0 3.6 dft.2
  3.6 6.6 all-to-all-start
  10.2 28.8 %dft.3 = (bf16[16,8,120,512]{3,2,1,0:T(8,128)(2,1)}, bf16[16,8,120,512]{3,2,1,0:T(8,128)(2,1)}) custom-call(bf16[128,512,256]{2,1,0:T(8,128)(2,1)} %traces_ref.3, bf16[256,256]{1,0:T(8,128)(2,1)} %constant.6.clone.table_ref), custom_call_target="tpu_custom_call" | custom-call | tf_op jit(solution)/shard_map/dft/pallas_call | solution.py:83
  39.0 18.7 %all-to-all-done.refs_0_ = bf16[16,16,8,512]{3,2,1,0:T(8,128)(2,1)} async-done(((bf16[16,16,8,512]{3,2,1,0:T(8,128)(2,1)}), bf16[16,16,8,512]{3,2,1,0:T(8,128)(2,1)}, u32[]{:S(2)}, u32[]{:S(2)}) %all-to-all-start) | async-done | bytes 2097184 | tf_op jit(solution)/shard_map/all_to_all | solution.py:220
  57.7 344.8 %all_to_all.30.refs_1_ = bf16[16,8,120,512]{3,2,1,0:T(8,128)(2,1)} all-to-all(bf16[16,8,120,512]{3,2,1,0:T(8,128)(2,1)} %get-tuple-element.13), channel_id=1, replica_groups=mesh['grp'=2,'band'=8,'rcv'=2] {'band','rcv'}, dimensions={0} | all-to-all | bytes 31457280 | tf_op jit(solution)/shard_map/all_to_all | solution.py:220
  402.5 6.1 all-to-all-start.1
  408.6 46.2 %square.3 = (bf16[16,8,8,512]{3,2,1,0:T(8,128)(2,1)}, bf16[16,8,120,512]{3,2,1,0:T(8,128)(2,1)}) custom-call(bf16[16,16,8,512]{3,2,1,0:T(8,128)(2,1)} %all-to-all-done.refs_0_, bf16[16,8,120,512]{3,2,1,0:T(8,128)(2,1)} %all_to_all.30.refs_1_), custom_call_target="tpu_custom_call" | custom-call | tf_op jit(solution)/shard_map/square/pallas_call | solution.py:137
  454.7 293.5 %all-to-all-done.1.refs_1_ = bf16[16,8,120,512]{3,2,1,0:T(8,128)(2,1)} async-done(((bf16[16,8,120,512]{3,2,1,0:T(8,128)(2,1)}), bf16[16,8,120,512]{3,2,1,0:T(8,128)(2,1)}, u32[]{:S(2)}, u32[]{:S(2)}) %all-to-all-start.1) | async-done | bytes 15728672 | tf_op jit(solution)/shard_map/all_to_all | solution.py:220
  748.2 5.0 all-to-all-start.5
  753.2 46.2 %square.2 = (bf16[16,8,8,512]{3,2,1,0:T(8,128)(2,1)}, bf16[16,8,120,512]{3,2,1,0:T(8,128)(2,1)}) custom-call(bf16[16,16,8,512]{3,2,1,0:T(8,128)(2,1)} %all-to-all-done.refs_0_, bf16[16,8,120,512]{3,2,1,0:T(8,128)(2,1)} %all-to-all-done.1.refs_1_), custom_call_target="tpu_custom_call" | custom-call | tf_op jit(solution)/shard_map/square/pallas_call | solution.py:137
  799.4 293.4 %all-to-all-done.5.refs_1_ = bf16[16,8,120,512]{3,2,1,0:T(8,128)(2,1)} async-done(((bf16[16,8,120,512]{3,2,1,0:T(8,128)(2,1)}), bf16[16,8,120,512]{3,2,1,0:T(8,128)(2,1)}, u32[]{:S(2)}, u32[]{:S(2)}) %all-to-all-start.5) | async-done | bytes 15728672 | tf_op jit(solution)/shard_map/all_to_all | solution.py:220
  1092.8 0.0 copy-start
  1092.8 0.0 copy-start.1
  1092.8 5.1 all-to-all-start.4
  1097.9 0.0 copy-done
  1097.9 0.0 copy-done.1
  1097.9 1.5 pad_maximum_fusion
  1099.4 338.0 %all-to-all-done.4.refs_0_ = bf16[16,8,120,512]{3,2,1,0:T(8,128)(2,1)} async-done(((bf16[16,8,120,512]{3,2,1,0:T(8,128)(2,1)}), bf16[16,8,120,512]{3,2,1,0:T(8,128)(2,1)}, u32[]{:S(2)}, u32[]{:S(2)}) %all-to-all-start.4) | async-done | bytes 15728672 | tf_op jit(solution)/shard_map/all_to_all | solution.py:220
  1437.5 4.9 all-to-all-start.3
  1442.4 29.3 %inverse.2.refs_2_ = bf16[128,512,256]{2,1,0:T(8,128)(2,1)} custom-call(bf16[16,8,120,512]{3,2,1,0:T(8,128)(2,1)} %all-to-all-done.4.refs_0_, bf16[16,8,120,512]{3,2,1,0:T(8,128)(2,1)} %all-to-all-done.5.refs_1_, bf16[256,256]{1,0:T(8,128)(2,1)} %constant.7.clone.refs_2_), custom_call_target="tpu_custom_call" | custom-call | tf_op jit(solution)/shard_map/inverse/pallas_call | solution.py:206
  1471.7 18.2 %all-to-all-done.3.refs_0_ = bf16[16,16,8,512]{3,2,1,0:T(8,128)(2,1)} async-done(((bf16[16,16,8,512]{3,2,1,0:T(8,128)(2,1)}), bf16[16,16,8,512]{3,2,1,0:T(8,128)(2,1)}, u32[]{:S(2)}, u32[]{:S(2)}) %all-to-all-start.3) | async-done | bytes 2097184 | tf_op jit(solution)/shard_map/all_to_all | solution.py:220
  1489.9 3.6 inverse.3
Async XLA Ops:
  3.6 54.1 %all-to-all-start = ((bf16[16,16,8,512]{3,2,1,0:T(8,128)(2,1)}), bf16[16,16,8,512]{3,2,1,0:T(8,128)(2,1)}, u32[]{:S(2)}, u32[]{:S(2)}) async-start(bf16[16,16,8,512]{3,2,1,0:T(8,128)(2,1)} %dft.2), calls=%async_computation | async-start | bytes 4194304 | tf_op jit(solution)/shard_map/all_to_all | solution.py:220
  402.5 345.7 %all-to-all-start.1 = ((bf16[16,8,120,512]{3,2,1,0:T(8,128)(2,1)}), bf16[16,8,120,512]{3,2,1,0:T(8,128)(2,1)}, u32[]{:S(2)}, u32[]{:S(2)}) async-start(bf16[16,8,120,512]{3,2,1,0:T(8,128)(2,1)} %get-tuple-element.11), calls=%async_computation.1 | async-start | bytes 31457280 | tf_op jit(solution)/shard_map/all_to_all | solution.py:220
  748.2 344.6 %all-to-all-start.5 = ((bf16[16,8,120,512]{3,2,1,0:T(8,128)(2,1)}), bf16[16,8,120,512]{3,2,1,0:T(8,128)(2,1)}, u32[]{:S(2)}, u32[]{:S(2)}) async-start(bf16[16,8,120,512]{3,2,1,0:T(8,128)(2,1)} %get-tuple-element.16), calls=%async_computation.5 | async-start | bytes 31457280 | tf_op jit(solution)/shard_map/all_to_all | solution.py:220
  1092.8 5.1 copy-start
  1092.8 5.1 copy-start.1
  1092.8 344.7 %all-to-all-start.4 = ((bf16[16,8,120,512]{3,2,1,0:T(8,128)(2,1)}), bf16[16,8,120,512]{3,2,1,0:T(8,128)(2,1)}, u32[]{:S(2)}, u32[]{:S(2)}) async-start(bf16[16,8,120,512]{3,2,1,0:T(8,128)(2,1)} %get-tuple-element.15), calls=%async_computation.4 | async-start | bytes 31457280 | tf_op jit(solution)/shard_map/all_to_all | solution.py:220
  1437.5 52.4 %all-to-all-start.3 = ((bf16[16,16,8,512]{3,2,1,0:T(8,128)(2,1)}), bf16[16,16,8,512]{3,2,1,0:T(8,128)(2,1)}, u32[]{:S(2)}, u32[]{:S(2)}) async-start(bf16[16,16,8,512]{3,2,1,0:T(8,128)(2,1)} %pad_maximum_fusion), calls=%async_computation.3 | async-start | bytes 4194304 | tf_op jit(solution)/shard_map/all_to_all | solution.py:220

commit v5 on v4

--- a/solution.py
+++ b/solution.py
@@ -77,7 +77,8 @@
 def dft(traces, table, first, count, rows, owners, chunks):
     _, receivers, length = traces.shape
     lanes = min(LANES, receivers)
-    width = length // (owners * chunks)
+    channels = table.shape[0]
+    width = channels // (owners * chunks)
     out = jax.ShapeDtypeStruct((owners, width, count * rows, receivers), jnp.bfloat16)
     out_spec = pl.BlockSpec((owners, width, rows, lanes), lambda i, j: (0, 0, i, j))
     return pl.pallas_call(
@@ -85,11 +86,11 @@
         grid=(count, receivers // lanes),
         in_specs=[
             pl.BlockSpec((rows, lanes, length), lambda i, j: (i + first, j, 0)),
-            pl.BlockSpec((length, length), lambda i, j: (0, 0)),
+            pl.BlockSpec((channels, length), lambda i, j: (0, 0)),
         ],
         out_specs=[out_spec] * chunks,
         out_shape=[out] * chunks,
-        scratch_shapes=[pltpu.VMEM((lanes // TILE, length * rows, TILE), jnp.float32)],
+        scratch_shapes=[pltpu.VMEM((lanes // TILE, channels * rows, TILE), jnp.float32)],
         compiler_params=pltpu.CompilerParams(vmem_limit_bytes=VMEM),
         name="dft",
     )(traces, table)
@@ -229,7 +230,10 @@
     rest_count = sources - SLAB
     (slab,) = dft(traces, table, rest_count // SLAB, 1, SLAB, owners, 1)
     slab = exchange(slab)
-    rest = dft(traces, table, 0, rest_count // BLOCK, BLOCK, owners, CHUNKS)
+    rest = []
+    for part in np.split(table.reshape(owners, -1, length), CHUNKS, axis=1):
+        part = part.reshape(length // CHUNKS, length)
+        rest += dft(traces, part, 0, rest_count // BLOCK, BLOCK, owners, 1)
     rest = [exchange(part) for part in rest]
     slab_parts, rest_parts = [], []
     for chunk in range(CHUNKS):

time: 1490 us -> 1490 us (level)
  blocking collectives: 345 us -> 0 us
  waiting for transfers between devices: 962 us -> 1280 us
  Pallas kernels: 158 us -> 176 us
    all_to_all x1 -> x0, blocking collectives: 345 us -> none  [exchange(): return lax.all_to_all(array, OWNERS, 0, 0)]
    all_to_all x5 -> x6, waiting for transfers between devices: 962 us -> 1280 us  [exchange(): return lax.all_to_all(array, OWNERS, 0, 0)]
    pallas_call x2 -> x3, Pallas kernels: 32.5 us -> 51 us  [dft(): pl.pallas_call(dft_kernel, grid=(count, receivers // lanes), in_specs=[pl...]
    all_to_all x5 -> x6, starting transfers between devices: 27.6 us -> 31.5 us  [exchange(): return lax.all_to_all(array, OWNERS, 0, 0)]
  transfers between devices with their start and end apart: 5 -> 6, of which waited for: 5 -> 6; matrix products, arithmetic and copies ran while one was open for 0% -> 0% of each run, Pallas kernels for 10% -> 11%
where the time goes in v5:
time: 1490 us
  waiting for transfers between devices  1280 us (86%)
  Pallas kernels  176 us (12%)
  starting transfers between devices  31.5 us (2%)
    all_to_all x6, waiting for transfers between devices, exchange(): return lax.all_to_all(array, OWNERS, 0, 0)  1280 us
    pallas_call x2, Pallas kernels, square(): pl.pallas_call(kernel, grid=(freqs,), in_specs=[pl.BlockSpec((owners, 2,...  92.4 us
    pallas_call x3, Pallas kernels, dft(): pl.pallas_call(dft_kernel, grid=(count, receivers // lanes), in_specs=[pl...  51 us
    pallas_call x2, Pallas kernels, inverse_transform(): pl.pallas_call(kernel, grid=(total // rows, receivers // lanes), in_specs...  32.9 us
    all_to_all x6, starting transfers between devices, exchange(): return lax.all_to_all(array, OWNERS, 0, 0)  31.5 us
  transfers between devices with their start and end apart: 6, of which 6 were waited for; matrix products, arithmetic and copies ran while one was open for 0% of the time, Pallas kernels for 11%

profile of v5, /device:TPU:11, one launch (start us, length us, event | category | flops | bytes accessed | tf_op | source)
XLA Modules:
  0.0 1492.1 jit_solution(8318183063608609132)
XLA Ops:
  0.0 3.6 dft.3
  3.6 6.6 all-to-all-start
  10.2 23.7 %dft.4 = bf16[16,8,120,512]{3,2,1,0:T(8,128)(2,1)} custom-call(bf16[128,512,256]{2,1,0:T(8,128)(2,1)} %traces_ref.5, bf16[128,256]{1,0:T(8,128)(2,1)} %constant.11.clone.table_ref), custom_call_target="tpu_custom_call" | custom-call | tf_op jit(solution)/shard_map/dft/pallas_call | solution.py:84
  33.9 23.8 %all-to-all-done.refs_0_ = bf16[16,16,8,512]{3,2,1,0:T(8,128)(2,1)} async-done(((bf16[16,16,8,512]{3,2,1,0:T(8,128)(2,1)}), bf16[16,16,8,512]{3,2,1,0:T(8,128)(2,1)}, u32[]{:S(2)}, u32[]{:S(2)}) %all-to-all-start) | async-done | bytes 2097184 | tf_op jit(solution)/shard_map/all_to_all | solution.py:221
  57.7 5.0 all-to-all-start.1
  62.7 23.7 %dft.5 = bf16[16,8,120,512]{3,2,1,0:T(8,128)(2,1)} custom-call(bf16[128,512,256]{2,1,0:T(8,128)(2,1)} %traces_ref.5, bf16[128,256]{1,0:T(8,128)(2,1)} %constant.12.clone.table_ref), custom_call_target="tpu_custom_call" | custom-call | tf_op jit(solution)/shard_map/dft/pallas_call | solution.py:84
  86.4 315.9 %all-to-all-done.1.refs_1_ = bf16[16,8,120,512]{3,2,1,0:T(8,128)(2,1)} async-done(((bf16[16,8,120,512]{3,2,1,0:T(8,128)(2,1)}), bf16[16,8,120,512]{3,2,1,0:T(8,128)(2,1)}, u32[]{:S(2)}, u32[]{:S(2)}) %all-to-all-start.1) | async-done | bytes 15728672 | tf_op jit(solution)/shard_map/all_to_all | solution.py:221
  402.2 5.0 all-to-all-start.2
  407.2 46.2 %square.2 = (bf16[16,8,8,512]{3,2,1,0:T(8,128)(2,1)}, bf16[16,8,120,512]{3,2,1,0:T(8,128)(2,1)}) custom-call(bf16[16,16,8,512]{3,2,1,0:T(8,128)(2,1)} %all-to-all-done.refs_0_, bf16[16,8,120,512]{3,2,1,0:T(8,128)(2,1)} %all-to-all-done.1.refs_1_), custom_call_target="tpu_custom_call" | custom-call | tf_op jit(solution)/shard_map/square/pallas_call | solution.py:138
  453.4 293.4 %all-to-all-done.2.refs_1_ = bf16[16,8,120,512]{3,2,1,0:T(8,128)(2,1)} async-done(((bf16[16,8,120,512]{3,2,1,0:T(8,128)(2,1)}), bf16[16,8,120,512]{3,2,1,0:T(8,128)(2,1)}, u32[]{:S(2)}, u32[]{:S(2)}) %all-to-all-start.2) | async-done | bytes 15728672 | tf_op jit(solution)/shard_map/all_to_all | solution.py:221
  746.8 5.0 all-to-all-start.4
  751.8 46.2 %square.3 = (bf16[16,8,8,512]{3,2,1,0:T(8,128)(2,1)}, bf16[16,8,120,512]{3,2,1,0:T(8,128)(2,1)}) custom-call(bf16[16,16,8,512]{3,2,1,0:T(8,128)(2,1)} %all-to-all-done.refs_0_, bf16[16,8,120,512]{3,2,1,0:T(8,128)(2,1)} %all-to-all-done.2.refs_1_), custom_call_target="tpu_custom_call" | custom-call | tf_op jit(solution)/shard_map/square/pallas_call | solution.py:138
  798.0 293.4 %all-to-all-done.4.refs_0_ = bf16[16,8,120,512]{3,2,1,0:T(8,128)(2,1)} async-done(((bf16[16,8,120,512]{3,2,1,0:T(8,128)(2,1)}), bf16[16,8,120,512]{3,2,1,0:T(8,128)(2,1)}, u32[]{:S(2)}, u32[]{:S(2)}) %all-to-all-start.4) | async-done | bytes 15728672 | tf_op jit(solution)/shard_map/all_to_all | solution.py:221
  1091.3 0.0 copy-start
  1091.3 0.0 copy-start.1
  1091.4 5.1 all-to-all-start.5
  1096.5 0.0 copy-done
  1096.5 0.0 copy-done.1
  1096.5 1.5 pad_maximum_fusion
  1098.0 338.0 %all-to-all-done.5.refs_1_ = bf16[16,8,120,512]{3,2,1,0:T(8,128)(2,1)} async-done(((bf16[16,8,120,512]{3,2,1,0:T(8,128)(2,1)}), bf16[16,8,120,512]{3,2,1,0:T(8,128)(2,1)}, u32[]{:S(2)}, u32[]{:S(2)}) %all-to-all-start.5) | async-done | bytes 15728672 | tf_op jit(solution)/shard_map/all_to_all | solution.py:221
  1436.0 4.9 all-to-all-start.3
  1440.9 29.3 %inverse.2.refs_2_ = bf16[128,512,256]{2,1,0:T(8,128)(2,1)} custom-call(bf16[16,8,120,512]{3,2,1,0:T(8,128)(2,1)} %all-to-all-done.4.refs_0_, bf16[16,8,120,512]{3,2,1,0:T(8,128)(2,1)} %all-to-all-done.5.refs_1_, bf16[256,256]{1,0:T(8,128)(2,1)} %constant.13.clone.refs_2_), custom_call_target="tpu_custom_call" | custom-call | tf_op jit(solution)/shard_map/inverse/pallas_call | solution.py:207
  1470.2 18.2 %all-to-all-done.3.refs_0_ = bf16[16,16,8,512]{3,2,1,0:T(8,128)(2,1)} async-done(((bf16[16,16,8,512]{3,2,1,0:T(8,128)(2,1)}), bf16[16,16,8,512]{3,2,1,0:T(8,128)(2,1)}, u32[]{:S(2)}, u32[]{:S(2)}) %all-to-all-start.3) | async-done | bytes 2097184 | tf_op jit(solution)/shard_map/all_to_all | solution.py:221
  1488.5 3.6 inverse.3
Async XLA Ops:
  3.6 54.1 %all-to-all-start = ((bf16[16,16,8,512]{3,2,1,0:T(8,128)(2,1)}), bf16[16,16,8,512]{3,2,1,0:T(8,128)(2,1)}, u32[]{:S(2)}, u32[]{:S(2)}) async-start(bf16[16,16,8,512]{3,2,1,0:T(8,128)(2,1)} %dft.3), calls=%async_computation | async-start | bytes 4194304 | tf_op jit(solution)/shard_map/all_to_all | solution.py:221
  57.7 344.6 %all-to-all-start.1 = ((bf16[16,8,120,512]{3,2,1,0:T(8,128)(2,1)}), bf16[16,8,120,512]{3,2,1,0:T(8,128)(2,1)}, u32[]{:S(2)}, u32[]{:S(2)}) async-start(bf16[16,8,120,512]{3,2,1,0:T(8,128)(2,1)} %dft.4), calls=%async_computation.1 | async-start | bytes 31457280 | tf_op jit(solution)/shard_map/all_to_all | solution.py:221
  402.2 344.6 %all-to-all-start.2 = ((bf16[16,8,120,512]{3,2,1,0:T(8,128)(2,1)}), bf16[16,8,120,512]{3,2,1,0:T(8,128)(2,1)}, u32[]{:S(2)}, u32[]{:S(2)}) async-start(bf16[16,8,120,512]{3,2,1,0:T(8,128)(2,1)} %dft.5), calls=%async_computation.2 | async-start | bytes 31457280 | tf_op jit(solution)/shard_map/all_to_all | solution.py:221
  746.8 344.6 %all-to-all-start.4 = ((bf16[16,8,120,512]{3,2,1,0:T(8,128)(2,1)}), bf16[16,8,120,512]{3,2,1,0:T(8,128)(2,1)}, u32[]{:S(2)}, u32[]{:S(2)}) async-start(bf16[16,8,120,512]{3,2,1,0:T(8,128)(2,1)} %get-tuple-element.11), calls=%async_computation.4 | async-start | bytes 31457280 | tf_op jit(solution)/shard_map/all_to_all | solution.py:221
  1091.3 5.1 copy-start
  1091.3 5.1 copy-start.1
  1091.4 344.7 %all-to-all-start.5 = ((bf16[16,8,120,512]{3,2,1,0:T(8,128)(2,1)}), bf16[16,8,120,512]{3,2,1,0:T(8,128)(2,1)}, u32[]{:S(2)}, u32[]{:S(2)}) async-start(bf16[16,8,120,512]{3,2,1,0:T(8,128)(2,1)} %get-tuple-element.12), calls=%async_computation.5 | async-start | bytes 31457280 | tf_op jit(solution)/shard_map/all_to_all | solution.py:221
  1436.0 52.4 %all-to-all-start.3 = ((bf16[16,16,8,512]{3,2,1,0:T(8,128)(2,1)}), bf16[16,16,8,512]{3,2,1,0:T(8,128)(2,1)}, u32[]{:S(2)}, u32[]{:S(2)}) async-start(bf16[16,16,8,512]{3,2,1,0:T(8,128)(2,1)} %pad_maximum_fusion), calls=%async_computation.3 | async-start | bytes 4194304 | tf_op jit(solution)/shard_map/all_to_all | solution.py:221

commit v6 on v5

--- a/solution.py
+++ b/solution.py
@@ -71,7 +71,7 @@
                     out[owner, c, :, lanes] = scratch[k, pl.ds(row, sources), :].astype(jnp.bfloat16)
         return carry
 
-    lax.fori_loop(0, owners, regroup, 0, unroll=4)
+    lax.fori_loop(0, owners, regroup, 0, unroll=16)
 
 
 def dft(traces, table, first, count, rows, owners, chunks):
@@ -168,7 +168,7 @@
                     scratch[k, pl.ds(row, sources), :] = block[:, window]
             return carry
 
-        lax.fori_loop(0, owners, widen, 0, unroll=2)
+        lax.fori_loop(0, owners, widen, 0, unroll=4)
 
     def transform(s, carry):
         total = jnp.concatenate(

time: 1490 us -> 1490 us (level)
  no operation moved by 1% of the time
where the time goes in v6:
time: 1490 us
  waiting for transfers between devices  1280 us (86%)
  Pallas kernels  176 us (12%)
  starting transfers between devices  31.5 us (2%)
    all_to_all x6, waiting for transfers between devices, exchange(): return lax.all_to_all(array, OWNERS, 0, 0)  1280 us
    pallas_call x2, Pallas kernels, square(): pl.pallas_call(kernel, grid=(freqs,), in_specs=[pl.BlockSpec((owners, 2,...  92.4 us
    pallas_call x3, Pallas kernels, dft(): pl.pallas_call(dft_kernel, grid=(count, receivers // lanes), in_specs=[pl...  50.7 us
    pallas_call x2, Pallas kernels, inverse_transform(): pl.pallas_call(kernel, grid=(total // rows, receivers // lanes), in_specs...  32.8 us
    all_to_all x6, starting transfers between devices, exchange(): return lax.all_to_all(array, OWNERS, 0, 0)  31.5 us
  transfers between devices with their start and end apart: 6, of which 6 were waited for; matrix products, arithmetic and copies ran while one was open for 0% of the time, Pallas kernels for 11%

profile of v6, /device:TPU:11, one launch (start us, length us, event | category | flops | bytes accessed | tf_op | source)
XLA Modules:
  0.0 1491.9 jit_solution(2696523272830951789)
XLA Ops:
  0.0 3.5 dft.3
  3.5 6.6 all-to-all-start
  10.0 23.6 %dft.4 = bf16[16,8,120,512]{3,2,1,0:T(8,128)(2,1)} custom-call(bf16[128,512,256]{2,1,0:T(8,128)(2,1)} %traces_ref.5, bf16[128,256]{1,0:T(8,128)(2,1)} %constant.11.clone.table_ref), custom_call_target="tpu_custom_call" | custom-call | tf_op jit(solution)/shard_map/dft/pallas_call | solution.py:84
  33.7 23.9 %all-to-all-done.refs_0_ = bf16[16,16,8,512]{3,2,1,0:T(8,128)(2,1)} async-done(((bf16[16,16,8,512]{3,2,1,0:T(8,128)(2,1)}), bf16[16,16,8,512]{3,2,1,0:T(8,128)(2,1)}, u32[]{:S(2)}, u32[]{:S(2)}) %all-to-all-start) | async-done | bytes 2097184 | tf_op jit(solution)/shard_map/all_to_all | solution.py:221
  57.5 5.0 all-to-all-start.1
  62.5 23.6 %dft.5 = bf16[16,8,120,512]{3,2,1,0:T(8,128)(2,1)} custom-call(bf16[128,512,256]{2,1,0:T(8,128)(2,1)} %traces_ref.5, bf16[128,256]{1,0:T(8,128)(2,1)} %constant.12.clone.table_ref), custom_call_target="tpu_custom_call" | custom-call | tf_op jit(solution)/shard_map/dft/pallas_call | solution.py:84
  86.1 316.0 %all-to-all-done.1.refs_1_ = bf16[16,8,120,512]{3,2,1,0:T(8,128)(2,1)} async-done(((bf16[16,8,120,512]{3,2,1,0:T(8,128)(2,1)}), bf16[16,8,120,512]{3,2,1,0:T(8,128)(2,1)}, u32[]{:S(2)}, u32[]{:S(2)}) %all-to-all-start.1) | async-done | bytes 15728672 | tf_op jit(solution)/shard_map/all_to_all | solution.py:221
  402.1 5.0 all-to-all-start.2
  407.1 46.2 %square.2 = (bf16[16,8,8,512]{3,2,1,0:T(8,128)(2,1)}, bf16[16,8,120,512]{3,2,1,0:T(8,128)(2,1)}) custom-call(bf16[16,16,8,512]{3,2,1,0:T(8,128)(2,1)} %all-to-all-done.refs_0_, bf16[16,8,120,512]{3,2,1,0:T(8,128)(2,1)} %all-to-all-done.1.refs_1_), custom_call_target="tpu_custom_call" | custom-call | tf_op jit(solution)/shard_map/square/pallas_call | solution.py:138
  453.3 293.4 %all-to-all-done.2.refs_1_ = bf16[16,8,120,512]{3,2,1,0:T(8,128)(2,1)} async-done(((bf16[16,8,120,512]{3,2,1,0:T(8,128)(2,1)}), bf16[16,8,120,512]{3,2,1,0:T(8,128)(2,1)}, u32[]{:S(2)}, u32[]{:S(2)}) %all-to-all-start.2) | async-done | bytes 15728672 | tf_op jit(solution)/shard_map/all_to_all | solution.py:221
  746.6 5.0 all-to-all-start.4
  751.6 46.2 %square.3 = (bf16[16,8,8,512]{3,2,1,0:T(8,128)(2,1)}, bf16[16,8,120,512]{3,2,1,0:T(8,128)(2,1)}) custom-call(bf16[16,16,8,512]{3,2,1,0:T(8,128)(2,1)} %all-to-all-done.refs_0_, bf16[16,8,120,512]{3,2,1,0:T(8,128)(2,1)} %all-to-all-done.2.refs_1_), custom_call_target="tpu_custom_call" | custom-call | tf_op jit(solution)/shard_map/square/pallas_call | solution.py:138
  797.8 293.4 %all-to-all-done.4.refs_0_ = bf16[16,8,120,512]{3,2,1,0:T(8,128)(2,1)} async-done(((bf16[16,8,120,512]{3,2,1,0:T(8,128)(2,1)}), bf16[16,8,120,512]{3,2,1,0:T(8,128)(2,1)}, u32[]{:S(2)}, u32[]{:S(2)}) %all-to-all-start.4) | async-done | bytes 15728672 | tf_op jit(solution)/shard_map/all_to_all | solution.py:221
  1091.2 0.0 copy-start
  1091.2 0.0 copy-start.1
  1091.2 5.1 all-to-all-start.5
  1096.3 0.0 copy-done
  1096.3 0.0 copy-done.1
  1096.3 1.5 pad_maximum_fusion
  1097.8 338.0 %all-to-all-done.5.refs_1_ = bf16[16,8,120,512]{3,2,1,0:T(8,128)(2,1)} async-done(((bf16[16,8,120,512]{3,2,1,0:T(8,128)(2,1)}), bf16[16,8,120,512]{3,2,1,0:T(8,128)(2,1)}, u32[]{:S(2)}, u32[]{:S(2)}) %all-to-all-start.5) | async-done | bytes 15728672 | tf_op jit(solution)/shard_map/all_to_all | solution.py:221
  1435.9 4.9 all-to-all-start.3
  1440.8 29.2 %inverse.2.refs_2_ = bf16[128,512,256]{2,1,0:T(8,128)(2,1)} custom-call(bf16[16,8,120,512]{3,2,1,0:T(8,128)(2,1)} %all-to-all-done.4.refs_0_, bf16[16,8,120,512]{3,2,1,0:T(8,128)(2,1)} %all-to-all-done.5.refs_1_, bf16[256,256]{1,0:T(8,128)(2,1)} %constant.13.clone.refs_2_), custom_call_target="tpu_custom_call" | custom-call | tf_op jit(solution)/shard_map/inverse/pallas_call | solution.py:207
  1470.0 18.4 %all-to-all-done.3.refs_0_ = bf16[16,16,8,512]{3,2,1,0:T(8,128)(2,1)} async-done(((bf16[16,16,8,512]{3,2,1,0:T(8,128)(2,1)}), bf16[16,16,8,512]{3,2,1,0:T(8,128)(2,1)}, u32[]{:S(2)}, u32[]{:S(2)}) %all-to-all-start.3) | async-done | bytes 2097184 | tf_op jit(solution)/shard_map/all_to_all | solution.py:221
  1488.3 3.6 inverse.3
Async XLA Ops:
  3.5 54.1 %all-to-all-start = ((bf16[16,16,8,512]{3,2,1,0:T(8,128)(2,1)}), bf16[16,16,8,512]{3,2,1,0:T(8,128)(2,1)}, u32[]{:S(2)}, u32[]{:S(2)}) async-start(bf16[16,16,8,512]{3,2,1,0:T(8,128)(2,1)} %dft.3), calls=%async_computation | async-start | bytes 4194304 | tf_op jit(solution)/shard_map/all_to_all | solution.py:221
  57.5 344.6 %all-to-all-start.1 = ((bf16[16,8,120,512]{3,2,1,0:T(8,128)(2,1)}), bf16[16,8,120,512]{3,2,1,0:T(8,128)(2,1)}, u32[]{:S(2)}, u32[]{:S(2)}) async-start(bf16[16,8,120,512]{3,2,1,0:T(8,128)(2,1)} %dft.4), calls=%async_computation.1 | async-start | bytes 31457280 | tf_op jit(solution)/shard_map/all_to_all | solution.py:221
  402.1 344.6 %all-to-all-start.2 = ((bf16[16,8,120,512]{3,2,1,0:T(8,128)(2,1)}), bf16[16,8,120,512]{3,2,1,0:T(8,128)(2,1)}, u32[]{:S(2)}, u32[]{:S(2)}) async-start(bf16[16,8,120,512]{3,2,1,0:T(8,128)(2,1)} %dft.5), calls=%async_computation.2 | async-start | bytes 31457280 | tf_op jit(solution)/shard_map/all_to_all | solution.py:221
  746.6 344.6 %all-to-all-start.4 = ((bf16[16,8,120,512]{3,2,1,0:T(8,128)(2,1)}), bf16[16,8,120,512]{3,2,1,0:T(8,128)(2,1)}, u32[]{:S(2)}, u32[]{:S(2)}) async-start(bf16[16,8,120,512]{3,2,1,0:T(8,128)(2,1)} %get-tuple-element.11), calls=%async_computation.4 | async-start | bytes 31457280 | tf_op jit(solution)/shard_map/all_to_all | solution.py:221
  1091.2 5.1 copy-start
  1091.2 5.1 copy-start.1
  1091.2 344.7 %all-to-all-start.5 = ((bf16[16,8,120,512]{3,2,1,0:T(8,128)(2,1)}), bf16[16,8,120,512]{3,2,1,0:T(8,128)(2,1)}, u32[]{:S(2)}, u32[]{:S(2)}) async-start(bf16[16,8,120,512]{3,2,1,0:T(8,128)(2,1)} %get-tuple-element.12), calls=%async_computation.5 | async-start | bytes 31457280 | tf_op jit(solution)/shard_map/all_to_all | solution.py:221
  1435.9 52.4 %all-to-all-start.3 = ((bf16[16,16,8,512]{3,2,1,0:T(8,128)(2,1)}), bf16[16,16,8,512]{3,2,1,0:T(8,128)(2,1)}, u32[]{:S(2)}, u32[]{:S(2)}) async-start(bf16[16,16,8,512]{3,2,1,0:T(8,128)(2,1)} %pad_maximum_fusion), calls=%async_computation.3 | async-start | bytes 4194304 | tf_op jit(solution)/shard_map/all_to_all | solution.py:221
